TPU v7x, 32 devices: a whole 2x2x4 slice. The times are simulated.
32 devices in a mesh: wide: 8 (over z, y), narrow: 4 (over x, core).
Axes of the slice: x: 2, y: 2, z: 4, core: 2. Of those that a mesh axis runs over, the one named last changes fastest.
Arguments:
- media_feats: bfloat16 [8, 2048, 1536], P('wide', 'narrow'), may hold values from -6 to 6
- latents: bfloat16 [8, 64, 1536], P('wide', 'narrow'), may hold values from -6 to 6
- frame_counts: int32 [8], P('wide'), may hold values from 1 to 8, as said below
- media_mask: int32 [8, 2048], P('wide'), may hold values 0 or 1
- time_embed: bfloat16 [8, 1536], replicated, may hold values from -3 to 3
- media_gain: float32 [1536], replicated, may hold values from 0.1 to 1.9
- media_bias: float32 [1536], replicated, may hold values from -1.75 to 1.75
- latent_gain: float32 [1536], replicated, may hold values from 0.1 to 1.9
- latent_bias: float32 [1536], replicated, may hold values from -1.75 to 1.75
- ffn_gain: float32 [1536], replicated, may hold values from 0.1 to 1.9
- ffn_bias: float32 [1536], replicated, may hold values from -1.75 to 1.75
- query_weight: bfloat16 [1536, 1536], P('wide', 'narrow'), may hold values from -0.3125 to 0.3125
- keyval_weight: bfloat16 [1536, 2, 1536], P('wide', None, 'narrow'), may hold values from -0.15625 to 0.15625
- output_weight: bfloat16 [1536, 1536], P('narrow', 'wide'), may hold values from -0.625 to 0.625
- up_weight: bfloat16 [1536, 6144], P(None, 'narrow'), may hold values from -0.15625 to 0.15625
- down_weight: bfloat16 [6144, 1536], P('narrow'), may hold values from -0.078125 to 0.078125
- cotangent: bfloat16 [8, 64, 1536], P('wide', 'narrow'), may hold values from -6 to 6
Outputs:
- out_latents: bfloat16 [8, 64, 1536], P('wide', 'narrow')
- grad_media: bfloat16 [8, 2048, 1536], P('wide', 'narrow')
- grad_latents: bfloat16 [8, 64, 1536], P('wide', 'narrow')
- grad_time_embed: float32 [8, 1536], P(None, ('wide', 'narrow'))
- grad_media_gain: float32 [1536], P(('wide', 'narrow'))
- grad_media_bias: float32 [1536], P(('wide', 'narrow'))
- grad_latent_gain: float32 [1536], P(('wide', 'narrow'))
- grad_latent_bias: float32 [1536], P(('wide', 'narrow'))
- grad_ffn_gain: float32 [1536], P(('wide', 'narrow'))
- grad_ffn_bias: float32 [1536], P(('wide', 'narrow'))
- grad_query_weight: float32 [1536, 1536], P('wide', 'narrow')
- grad_keyval_weight: float32 [1536, 2, 1536], P('wide', None, 'narrow')
- grad_output_weight: float32 [1536, 1536], P('narrow', 'wide')
- grad_up_weight: float32 [1536, 6144], P('wide', 'narrow')
- grad_down_weight: float32 [6144, 1536], P('narrow', 'wide')
Inputs may be any that keep to these rules, and one draw needn't show every extreme that they name: `frame_counts`: frames of each item; some item has exactly 8.
All inputs are finite; a program needn't handle non-finite values. No bound on the sum of `media_mask` on one device may be relied on, other than what follows from the above.
Results may differ from a plain program's by a relative error of at most 0.02.
Values may be sent and summed in bfloat16 or wider, within the bound.
A program may use at most 128 MiB of HBM per device.

v0:
```python
import math

import jax
import jax.numpy as jnp
from jax import lax
from jax.sharding import PartitionSpec as P

HEADS = 16
HEAD_DIM = 96
FRAMES_MAX = 8
PATCHES = 256


EPS = 1e-05
ENT_COEF = 4.0
HIGH = lax.Precision.HIGHEST


def norm_forward(values, norm_gain, norm_bias):
    row_mean = jnp.mean(values, axis=-1, keepdims=True)
    centered = values - row_mean
    inv_std = lax.rsqrt(jnp.mean(centered * centered, axis=-1, keepdims=True) + EPS)
    normed = centered * inv_std
    return (normed * norm_gain + norm_bias, normed, inv_std)


def norm_backward(grad_out, normed, inv_std, norm_gain):
    scaled = grad_out * norm_gain
    grad_in = inv_std * (
        scaled
        - jnp.mean(scaled, axis=-1, keepdims=True)
        - normed * jnp.mean(scaled * normed, axis=-1, keepdims=True)
    )
    return (grad_in, jnp.sum(grad_out * normed, axis=0), jnp.sum(grad_out, axis=0))


def gelu_slope(pre_act):
    cdf_part = 0.5 * (1.0 + lax.erf(pre_act * (1.0 / math.sqrt(2.0))))
    density = jnp.exp(-0.5 * pre_act * pre_act) * (1.0 / math.sqrt(2.0 * math.pi))
    return cdf_part + pre_act * density


def body(
    media_feats,
    latents,
    frame_counts,
    media_mask,
    time_embed,
    media_gain,
    media_bias,
    latent_gain,
    latent_bias,
    ffn_gain,
    ffn_bias,
    query_weight,
    keyval_weight,
    output_weight,
    up_weight,
    down_weight,
    cotangent,
):
    item_count = media_feats.shape[0]
    own_media = media_feats.shape[1]
    width = media_feats.shape[2]
    own_latent = latents.shape[1]
    narrow_size = lax.axis_size("narrow")
    narrow_pos = lax.axis_index("narrow")
    media_total = own_media * narrow_size
    latent_total = own_latent * narrow_size
    head_local = HEADS // narrow_size
    cols = head_local * HEAD_DIM
    key_total = media_total + latent_total
    all_ids = jnp.arange(media_total, dtype=jnp.int32) // PATCHES
    valid_tok = (all_ids[None, :] < frame_counts[:, None]) & (media_mask > 0)
    local_count = jnp.sum(valid_tok.astype(jnp.float32)) + float(item_count * latent_total)
    total_count = lax.psum(local_count, "wide")
    all_items = item_count * lax.axis_size("wide")
    ent_weight = ENT_COEF * float(all_items * media_total) / total_count
    query_own, keyval_own, output_own = (
        lax.all_gather(query_weight, "wide", axis=0, tiled=True),
        lax.all_gather(keyval_weight, "wide", axis=0, tiled=True),
        lax.all_gather(output_weight, "wide", axis=1, tiled=True),
    )
    query_full, keyval_full = (
        lax.all_gather(query_own, "narrow", axis=1, tiled=True),
        lax.all_gather(keyval_own, "narrow", axis=2, tiled=True),
    )
    keyval_flat = keyval_own.reshape(width, 2 * cols)
    own_ids = (narrow_pos * own_media + jnp.arange(own_media, dtype=jnp.int32)) // PATCHES
    frame_onehot = own_ids[:, None] == jnp.arange(FRAMES_MAX, dtype=jnp.int32)[None, :]
    time_rows = jnp.dot(
        frame_onehot.astype(jnp.bfloat16), time_embed, preferred_element_type=jnp.float32
    )
    score_scale = HEAD_DIM ** (-0.5)

    def item_step(carry, item):
        (
            down_acc,
            up_acc,
            output_acc,
            keyval_acc,
            query_acc,
            mg_acc,
            mb_acc,
            lg_acc,
            lb_acc,
            fg_acc,
            fb_acc,
            time_acc,
        ) = carry
        media_one, latent_one, valid_one, cot_one = item
        media_nf, media_hat, media_istd = norm_forward(
            media_one.astype(jnp.float32) + time_rows, media_gain, media_bias
        )
        latent_f32 = latent_one.astype(jnp.float32)
        latent_nf, latent_hat, latent_istd = norm_forward(latent_f32, latent_gain, latent_bias)
        media_all, latent_all = (
            lax.all_gather(media_nf.astype(jnp.bfloat16), "narrow", axis=0, tiled=True),
            lax.all_gather(latent_nf.astype(jnp.bfloat16), "narrow", axis=0, tiled=True),
        )
        keys_in = jnp.concatenate([media_all, latent_all], axis=0)
        query_act = jnp.dot(latent_all, query_own, preferred_element_type=jnp.float32).astype(
            jnp.bfloat16
        )
        key_vals = jnp.dot(keys_in, keyval_flat, preferred_element_type=jnp.float32).astype(
            jnp.bfloat16
        )
        query_heads = query_act.reshape(latent_total, head_local, HEAD_DIM)
        key_heads = key_vals[:, :cols].reshape(key_total, head_local, HEAD_DIM)
        value_heads = key_vals[:, cols:].reshape(key_total, head_local, HEAD_DIM)
        key_valid = jnp.concatenate([valid_one, jnp.ones((latent_total,), dtype=bool)])
        scores = (
            jnp.einsum("lhd,khd->hlk", query_heads, key_heads, preferred_element_type=jnp.float32)
            * score_scale
        )
        open_keys = key_valid[None, None, :]
        masked = jnp.where(open_keys, scores, -1e30)
        row_top = jnp.max(masked, axis=-1)
        expo = jnp.exp(masked - row_top[..., None])
        prob_all = expo / jnp.sum(expo, axis=-1)[..., None]
        prob_low = prob_all.astype(jnp.bfloat16)
        plain_scores = jnp.where(open_keys, scores, 0.0)
        mean_score = jnp.sum(prob_all * plain_scores, axis=-1)
        attn_out = jnp.einsum(
            "hlk,khd->lhd", prob_low, value_heads, preferred_element_type=jnp.float32
        ).reshape(latent_total, cols)
        attn_low = attn_out.astype(jnp.bfloat16)
        branch_part = jnp.dot(attn_low, output_own, preferred_element_type=jnp.float32)
        branch_own = lax.psum_scatter(
            branch_part.astype(jnp.bfloat16), "narrow", scatter_dimension=0, tiled=True
        ).astype(jnp.float32)
        latent_mid = latent_f32 + branch_own
        hidden_f, hidden_hat, hidden_istd = norm_forward(latent_mid, ffn_gain, ffn_bias)
        hidden_all, cot_all = (
            lax.all_gather(hidden_f.astype(jnp.bfloat16), "narrow", axis=0, tiled=True),
            lax.all_gather(cot_one, "narrow", axis=0, tiled=True),
        )
        pre_act = jnp.dot(hidden_all, up_weight, preferred_element_type=jnp.float32)
        act_low = jax.nn.gelu(pre_act, approximate=False).astype(jnp.bfloat16)
        ffn_part = jnp.dot(act_low, down_weight, preferred_element_type=jnp.float32)
        ffn_own = lax.psum_scatter(
            ffn_part.astype(jnp.bfloat16), "narrow", scatter_dimension=0, tiled=True
        ).astype(jnp.float32)
        out_one = (latent_mid + ffn_own).astype(jnp.bfloat16)
        down_acc = down_acc + jnp.einsum(
            "lf,ld->fd", act_low, cot_all, preferred_element_type=jnp.float32
        )
        grad_act = jnp.einsum("ld,fd->lf", cot_all, down_weight, preferred_element_type=jnp.float32)
        grad_pre = (grad_act * gelu_slope(pre_act)).astype(jnp.bfloat16)
        up_acc = up_acc + jnp.einsum(
            "ld,lf->df", hidden_all, grad_pre, preferred_element_type=jnp.float32
        )
        hidden_part = jnp.einsum(
            "lf,df->ld", grad_pre, up_weight, preferred_element_type=jnp.float32
        )
        grad_hidden = lax.psum_scatter(
            hidden_part.astype(jnp.bfloat16), "narrow", scatter_dimension=0, tiled=True
        ).astype(jnp.float32)
        grad_norm, fg_part, fb_part = norm_backward(grad_hidden, hidden_hat, hidden_istd, ffn_gain)
        grad_mid = cot_one.astype(jnp.float32) + grad_norm
        grad_branch_all = lax.all_gather(
            grad_mid.astype(jnp.bfloat16), "narrow", axis=0, tiled=True
        )
        output_acc = output_acc + jnp.einsum(
            "lc,ld->cd", attn_low, grad_branch_all, preferred_element_type=jnp.float32
        )
        grad_attn = jnp.einsum(
            "ld,cd->lc", grad_branch_all, output_own, preferred_element_type=jnp.float32
        ).astype(jnp.bfloat16)
        row_dots = jnp.sum(
            (grad_attn.astype(jnp.float32) * attn_out).reshape(latent_total, head_local, HEAD_DIM),
            axis=-1,
        )
        shift_rows = (jnp.transpose(row_dots, (1, 0)) - ent_weight * mean_score)[..., None]
        grad_heads = grad_attn.reshape(latent_total, head_local, HEAD_DIM)
        grad_prob = jnp.einsum(
            "lhd,khd->hlk", grad_heads, value_heads, preferred_element_type=jnp.float32
        )
        grad_scores = (prob_all * (grad_prob - ent_weight * plain_scores - shift_rows)).astype(
            jnp.bfloat16
        )
        grad_values = jnp.einsum(
            "hlk,lhd->khd", prob_low, grad_heads, preferred_element_type=jnp.float32
        ).reshape(key_total, cols)
        grad_keys = (
            jnp.einsum(
                "hlk,lhd->khd", grad_scores, query_heads, preferred_element_type=jnp.float32
            ).reshape(key_total, cols)
            * score_scale
        )
        grad_query = (
            jnp.einsum(
                "hlk,khd->lhd", grad_scores, key_heads, preferred_element_type=jnp.float32
            ).reshape(latent_total, cols)
            * score_scale
        ).astype(jnp.bfloat16)
        grad_pairs = jnp.concatenate([grad_keys, grad_values], axis=-1).astype(jnp.bfloat16)
        keyval_acc = keyval_acc + jnp.einsum(
            "kd,ke->de", keys_in, grad_pairs, preferred_element_type=jnp.float32
        )
        query_acc = query_acc + jnp.einsum(
            "ld,lc->dc", latent_all, grad_query, preferred_element_type=jnp.float32
        )
        media_pairs = grad_pairs[:media_total].reshape(media_total, 2, cols)
        latent_pairs = jnp.concatenate(
            [
                grad_pairs[media_total:].reshape(latent_total, 2, cols),
                grad_query.reshape(latent_total, 1, cols),
            ],
            axis=1,
        )
        media_back, latent_back = (
            lax.all_to_all(media_pairs, "narrow", split_axis=0, concat_axis=2, tiled=True),
            lax.all_to_all(latent_pairs, "narrow", split_axis=0, concat_axis=2, tiled=True),
        )
        grad_media_rows = jnp.einsum(
            "rsc,dsc->rd", media_back, keyval_full, preferred_element_type=jnp.float32
        )
        grad_latent_normed = jnp.einsum(
            "rsc,dsc->rd", latent_back[:, :2], keyval_full, preferred_element_type=jnp.float32
        ) + jnp.einsum(
            "rc,dc->rd", latent_back[:, 2], query_full, preferred_element_type=jnp.float32
        )
        grad_media_in, mg_part, mb_part = norm_backward(
            grad_media_rows, media_hat, media_istd, media_gain
        )
        time_acc = time_acc + jnp.einsum(
            "mf,md->fd", frame_onehot.astype(jnp.float32), grad_media_in, precision=HIGH
        )
        grad_latent_in, lg_part, lb_part = norm_backward(
            grad_latent_normed, latent_hat, latent_istd, latent_gain
        )
        grad_latent_one = (grad_mid + grad_latent_in).astype(jnp.bfloat16)
        carry = (
            down_acc,
            up_acc,
            output_acc,
            keyval_acc,
            query_acc,
            mg_acc + mg_part,
            mb_acc + mb_part,
            lg_acc + lg_part,
            lb_acc + lb_part,
            fg_acc + fg_part,
            fb_acc + fb_part,
            time_acc,
        )
        return (carry, (out_one, grad_media_in.astype(jnp.bfloat16), grad_latent_one))

    ff_local = up_weight.shape[1]
    vector_zero = jnp.zeros((width,), jnp.float32)
    start = (
        jnp.zeros((ff_local, width), jnp.float32),
        jnp.zeros((width, ff_local), jnp.float32),
        jnp.zeros((cols, width), jnp.float32),
        jnp.zeros((width, 2 * cols), jnp.float32),
        jnp.zeros((width, cols), jnp.float32),
        vector_zero,
        vector_zero,
        vector_zero,
        vector_zero,
        vector_zero,
        vector_zero,
        jnp.zeros((FRAMES_MAX, width), jnp.float32),
    )
    totals, stacked = lax.scan(item_step, start, (media_feats, latents, valid_tok, cotangent))
    (
        down_acc,
        up_acc,
        output_acc,
        keyval_acc,
        query_acc,
        mg_acc,
        mb_acc,
        lg_acc,
        lb_acc,
        fg_acc,
        fb_acc,
        time_acc,
    ) = totals
    out_latents, grad_media, grad_latents = stacked
    up_sum, down_sum, query_sum, keyval_sum, output_sum = (
        lax.psum_scatter(
            up_acc.astype(jnp.bfloat16), "wide", scatter_dimension=0, tiled=True
        ).astype(jnp.float32),
        lax.psum_scatter(
            down_acc.astype(jnp.bfloat16), "wide", scatter_dimension=1, tiled=True
        ).astype(jnp.float32),
        lax.psum_scatter(
            query_acc.astype(jnp.bfloat16), "wide", scatter_dimension=0, tiled=True
        ).astype(jnp.float32),
        lax.psum_scatter(
            keyval_acc.reshape(width, 2, cols).astype(jnp.bfloat16),
            "wide",
            scatter_dimension=0,
            tiled=True,
        ).astype(jnp.float32),
        lax.psum_scatter(
            output_acc.astype(jnp.bfloat16), "wide", scatter_dimension=1, tiled=True
        ).astype(jnp.float32),
    )
    mg_sum, mb_sum, lg_sum, lb_sum, fg_sum, fb_sum, time_sum = (
        lax.psum_scatter(mg_acc, ("wide", "narrow"), scatter_dimension=0, tiled=True),
        lax.psum_scatter(mb_acc, ("wide", "narrow"), scatter_dimension=0, tiled=True),
        lax.psum_scatter(lg_acc, ("wide", "narrow"), scatter_dimension=0, tiled=True),
        lax.psum_scatter(lb_acc, ("wide", "narrow"), scatter_dimension=0, tiled=True),
        lax.psum_scatter(fg_acc, ("wide", "narrow"), scatter_dimension=0, tiled=True),
        lax.psum_scatter(fb_acc, ("wide", "narrow"), scatter_dimension=0, tiled=True),
        lax.psum_scatter(time_acc, ("wide", "narrow"), scatter_dimension=1, tiled=True),
    )
    return (
        out_latents,
        grad_media,
        grad_latents,
        time_sum,
        mg_sum,
        mb_sum,
        lg_sum,
        lb_sum,
        fg_sum,
        fb_sum,
        query_sum,
        keyval_sum,
        output_sum,
        up_sum,
        down_sum,
    )


def solution(mesh):
    placed = (
        P("wide", "narrow", None),
        P("wide", "narrow", None),
        P("wide"),
        P("wide", None),
        P(),
        P(),
        P(),
        P(),
        P(),
        P(),
        P(),
        P("wide", "narrow"),
        P("wide", None, "narrow"),
        P("narrow", "wide"),
        P(None, "narrow"),
        P("narrow", None),
        P("wide", "narrow", None),
    )
    return jax.shard_map(
        body,
        mesh=mesh,
        in_specs=placed,
        out_specs=(
            P("wide", "narrow", None),
            P("wide", "narrow", None),
            P("wide", "narrow", None),
            P(None, ("wide", "narrow")),
            P(("wide", "narrow")),
            P(("wide", "narrow")),
            P(("wide", "narrow")),
            P(("wide", "narrow")),
            P(("wide", "narrow")),
            P(("wide", "narrow")),
            P("wide", "narrow"),
            P("wide", None, "narrow"),
            P("narrow", "wide"),
            P("wide", "narrow"),
            P("narrow", "wide"),
        ),
        check_vma=False,
    )
```

profile of v0, /device:TPU:0, one launch (start us, length us, event | category | flops | bytes accessed | tf_op | source)
XLA Modules:
  0.0 941.4 jit_solution(12498868731809088327)
XLA Ops:
  15.3 6.9 all_gather.36
  23.6 30.5 %all-gather.12.cloned.1.call-done = bf16[1536,384]{1,0:T(8,128)(2,1)} async-done(((bf16[192,384]{1,0:T(8,128)(2,1)}), bf16[1536,384]{1,0:T(8,128)(2,1)}) %all-gather.12.cloned.1.call-update) | async-done | bytes 1179664 | tf_op jit(solution)/shard_map/all_gather | solution.py:80
  55.8 51.6 %all-gather.10.cloned.1.call-done = bf16[1536,2,384]{2,0,1:T(8,128)(2,1)} async-done(((bf16[192,2,384]{2,0,1:T(8,128)(2,1)}), bf16[1536,2,384]{2,0,1:T(8,128)(2,1)}) %all-gather.10.cloned.1.call-update) | async-done | bytes 2359312 | tf_op jit(solution)/shard_map/all_gather | solution.py:81
  107.4 4.3 copy.117
  111.7 42.8 %all-gather.8.cloned.1.call-done = bf16[2048,1536]{1,0:T(8,128)(2,1)} async-done(((bf16[512,1536]{1,0:T(8,128)(2,1)}), bf16[2048,1536]{1,0:T(8,128)(2,1)}) %all-gather.8.cloned.1.call-update) | async-done | bytes 6291472 | tf_op jit(solution)/shard_map/while/body/eval_jaxpr/all_gather | solution.py:118
  154.4 3.3 constant_dynamic-update-slice_fusion.1
  157.9 5.5 convolution_convert_fusion.2
  165.4 3.7 copy.119
  169.2 3.8 copy.118
  173.0 3.6 fusion.82
  176.6 3.0 convolution_bitcast_fusion.3
  181.3 16.3 %all-gather.14.cloned.1.call-done = bf16[384,1536]{0,1:T(8,128)(2,1)} async-done(((bf16[384,192]{0,1:T(8,128)(2,1)}), bf16[384,1536]{0,1:T(8,128)(2,1)}) %all-gather.14.cloned.1.call-update) | async-done | bytes 1179664 | tf_op jit(solution)/shard_map/all_gather | solution.py:82
  197.6 2.4 convolution_convert_fusion.9
  200.1 7.1 all-gather
  207.2 11.8 %reduce-scatter.11.cloned.1.call-done = bf16[16,1536]{1,0:T(8,128)(2,1)} async-done(((bf16[64,1536]{1,0:T(8,128)(2,1)}), bf16[16,1536]{1,0:T(8,128)(2,1)}) %reduce-scatter.11.cloned.1.call-update) | async-done | bytes 49168 | tf_op jit(solution)/shard_map/while/body/eval_jaxpr/reduce_scatter | solution.py:149
  221.9 5.6 all_gather.40
  228.2 3.3 fusion.85
  231.5 4.0 fusion.8
  236.2 4.6 convolution_convert_fusion.7
  241.6 19.1 %reduce-scatter.15.cloned.1.call-done = bf16[16,1536]{1,0:T(8,128)(2,1)} async-done(((bf16[64,1536]{1,0:T(8,128)(2,1)}), bf16[16,1536]{1,0:T(8,128)(2,1)}) %reduce-scatter.15.cloned.1.call-update) | async-done | bytes 49168 | tf_op jit(solution)/shard_map/while/body/eval_jaxpr/reduce_scatter | solution.py:176
  263.2 5.6 all_gather.42
  269.4 2.5 convolution_convert_fusion.5
  272.6 22.0 %psum.7 = f32[]{:T(128)} all-reduce(f32[]{:T(128)S(6)} %add.196), channel_id=1, replica_groups=mesh['wide'=8,'narrow'=4] {'wide'}, use_global_device_ids=true, to_apply=%region_14.15 | all-reduce | flops 1 | bytes 8 | tf_op jit(solution)/shard_map/psum | solution.py:76
  295.4 4.2 multiply_reduce_fusion.4
  304.1 3.6 fusion.6
  313.9 2.9 convolution_convert_fusion.3
  316.8 10.9 %convolution_convert_fusion.4 = bf16[1536,768]{0,1:T(8,128)(2,1)} fusion(bf16[2112,1536]{1,0:T(8,128)(2,1)} %copy-done.6, bf16[2112,384]{0,1:T(8,128)(2,1)S(1)} %bitcast.160, bf16[2112,384]{0,1:T(8,128)(2,1)S(1)} %bitcast.155), kind=kOutput, calls=%fused_computation.19 | convolution fusion | flops 4990500864 | bytes 12091392 | tf_op jit(solution)/shard_map/while/body/eval_jaxpr/kd,ke->de/dot_general | solution.py:218
  327.7 6.9 copy.135
  335.3 3.5 fusion.7
  338.8 8.7 copy.126
  347.6 4.7 all-to-all-start
  352.3 4.7 convolution_convert_fusion.8
  357.3 31.9 %all-to-all-done = bf16[2048,2,384]{2,1,0:T(2,128)(2,1)} async-done(((bf16[2048,2,384]{2,1,0:T(2,128)(2,1)}), bf16[2048,2,384]{2,1,0:T(2,128)(2,1)}, u32[]{:S(2)}, u32[]{:S(2)}) %all-to-all-start) | async-done | bytes 3145760 | tf_op jit(solution)/shard_map/while/body/eval_jaxpr/all_to_all | solution.py:233
  393.5 10.0 %multiply_reduce_fusion = (f32[1536]{0:T(1024)}, f32[512]{0:T(512)S(1)}, f32[512]{0:T(512)S(1)}, f32[1536]{0:T(1024)}, f32[512,1536]{1,0:T(8,128)S(1)}) fusion(f32[512,1536]{1,0:T(8,128)S(1)} %get-tuple-element.150, f32[512]{0:T(512)S(1)} %add_rsqrt_fusion, f32[512]{0:T(512)S(1)} %broadcast_multiply_fusion.2, f32[1536]{0:T(1024)S(1)} %copy-done.33, ...), kind=kOutput, calls=%fused_computation.23 | convolution fusion | flops 4838912000 | bytes 18900992 | tf_op jit(solution)/shard_map/while/body/eval_jaxpr/rsc,dsc->rd/dot_general | solution.py:236
  405.6 3.6 convolution_bitcast_fusion.1
  409.3 3.5 convolution_convert_fusion.1
  413.9 3.9 convolution_convert_fusion
  421.3 3.6 all-to-all-start.1
  426.2 3.8 all-to-all-done.1
  431.6 31.3 %reduce-scatter.17.cloned.1.call-done = bf16[192,384]{1,0:T(8,128)(2,1)} async-done(((bf16[1536,384]{1,0:T(8,128)(2,1)}), bf16[192,384]{1,0:T(8,128)(2,1)}) %reduce-scatter.17.cloned.1.call-update) | async-done | bytes 147472 | tf_op jit(solution)/shard_map/reduce_scatter | solution.py:309
  464.6 109.4 %all-reduce.11.cloned.1.call-done = bf16[1536,2,384]{2,1,0:T(2,128)(2,1)} async-done(((bf16[1536,2,384]{2,1,0:T(2,128)(2,1)}), bf16[1536,2,384]{2,1,0:T(2,128)(2,1)}) %all-reduce.11.cloned.1.call-update) | async-done | bytes 2359312
  576.0 6.2 convolution_bitcast_fusion.2
  582.3 29.8 %all-gather.18.cloned.1.call-done = bf16[1536,1536]{1,0:T(8,128)(2,1)} async-done(((bf16[1536,384]{1,0:T(8,128)(2,1)}), bf16[1536,1536]{1,0:T(8,128)(2,1)}) %all-gather.18.cloned.1.call-update) | async-done | bytes 4718608 | tf_op jit(solution)/shard_map/all_gather | solution.py:85
  612.1 3.8 fusion.53
  616.0 40.1 %all-reduce.8 = (f32[1536]{0:T(1024)S(1)}, f32[1536]{0:T(1024)S(1)}, f32[1536]{0:T(1024)S(1)}, f32[1536]{0:T(1024)S(1)}, f32[1536]{0:T(1024)S(1)}, /*index=5*/f32[1536]{0:T(1024)S(1)}) all-reduce(f32[1536]{0:T(1024)S(1)} %copy-done.46, f32[1536]{0:T(1024)S(1)} %copy-done.47, ...), channel_id=7, replica_groups=mesh['wide'=8,'narrow'=4] {'wide','narrow'}, use_global_device_ids=true, to_apply=%region_23.24.clone | all-reduce | flops 9216 | bytes 73728
  661.2 74.4 %reduce-scatter.25.cloned.1.call-done = f32[48,8]{1,0:T(8,128)} async-done(((f32[1536,8]{1,0:T(8,128)}), f32[48,8]{1,0:T(8,128)}) %reduce-scatter.25.cloned.1.call-update) | async-done | bytes 1552
  737.0 96.9 %reduce-scatter.21.cloned.1.call-done = bf16[192,1536]{1,0:T(8,128)(2,1)} async-done(((bf16[1536,1536]{1,0:T(8,128)(2,1)}), bf16[192,1536]{1,0:T(8,128)(2,1)}) %reduce-scatter.21.cloned.1.call-update) | async-done | bytes 589840 | tf_op jit(solution)/shard_map/reduce_scatter | solution.py:303
  836.0 96.6 %reduce-scatter.23.cloned.1.call-done = bf16[1536,192]{0,1:T(8,128)(2,1)} async-done(((bf16[1536,1536]{0,1:T(8,128)(2,1)}), bf16[1536,192]{0,1:T(8,128)(2,1)}) %reduce-scatter.23.cloned.1.call-update) | async-done | bytes 589840 | tf_op jit(solution)/shard_map/reduce_scatter | solution.py:306
  (218 shorter events, 61.9 us)
Async XLA Ops:
  7.2 46.9 %all-gather.12.cloned.1.call-start = ((), (), s32[]{:S(2)}) async-start(), calls=%async_computation.12 | async-start | bytes 1327104 | tf_op jit(solution)/shard_map/all_gather | solution.py:80
  7.9 99.4 %all-gather.10.cloned.1.call-start = ((), (), s32[]{:S(2)}) async-start(), calls=%async_computation.11 | async-start | bytes 2654208 | tf_op jit(solution)/shard_map/all_gather | solution.py:81
  9.7 144.7 %all-gather.8.cloned.1.call-start = ((), (), s32[]{:S(2)}) async-start(), calls=%async_computation.10 | async-start | bytes 7864320 | tf_op jit(solution)/shard_map/while/body/eval_jaxpr/all_gather | solution.py:118
  12.5 10.4 %copy-start.45 = (s32[1,2048]{1,0:T(1,128)S(1)}, s32[1,2048]{1,0:T(1,128)}, u32[]{:S(2)}) copy-start(s32[1,2048]{1,0:T(1,128)} %param.20) | copy-start | bytes 24580
  14.2 183.4 %all-gather.14.cloned.1.call-start = ((), (), s32[]{:S(2)}) async-start(), calls=%async_computation.13 | async-start | bytes 1327104 | tf_op jit(solution)/shard_map/all_gather | solution.py:82
  14.8 204.2 %reduce-scatter.11.cloned.1.call-start = ((), (), s32[]{:S(2)}) async-start(), calls=%async_computation.14 | async-start | bytes 245760 | tf_op jit(solution)/shard_map/while/body/eval_jaxpr/reduce_scatter | solution.py:149
  15.0 7.9 copy-start.39
  15.2 7.6 copy-start.48
  23.5 149.4 %copy-start.54 = (pred[2112]{0:T(1024)(128)(4,1)}, pred[2112]{0:T(1024)(128)(4,1)S(1)}, u32[]{:S(2)}) copy-start(pred[2112]{0:T(1024)(128)(4,1)S(1)} %concatenate.18) | copy-start | bytes 6340
  55.8 117.2 %copy-start.27 = (bf16[64,4,96]{2,1,0:T(4,128)(2,1)}, bf16[64,4,96]{2,1,0:T(4,128)(2,1)S(1)}, u32[]{:S(2)}) copy-start(bf16[64,4,96]{2,1,0:T(4,128)(2,1)S(1)} %reshape.235) | copy-start | bytes 147460
  176.6 127.5 %copy-start.57 = (f32[4,64]{1,0:T(4,128)}, f32[4,64]{1,0:T(4,128)S(1)}, u32[]{:S(2)}) copy-start(f32[4,64]{1,0:T(4,128)S(1)} %get-tuple-element.151) | copy-start | bytes 3076
  176.6 44.4 %copy-start.28 = (f32[1536]{0:T(1024)S(1)}, f32[1536]{0:T(1024)}, u32[]{:S(2)}) copy-start(f32[1536]{0:T(1024)} %param.26) | copy-start | bytes 18436
  176.6 44.4 %copy-start.44 = (f32[1536]{0:T(1024)S(1)}, f32[1536]{0:T(1024)}, u32[]{:S(2)}) copy-start(f32[1536]{0:T(1024)} %param.27) | copy-start | bytes 18436
  181.3 50.1 %copy-start.18 = (f32[64,384]{1,0:T(8,128)}, f32[64,384]{1,0:T(8,128)S(1)}, u32[]{:S(2)}) copy-start(f32[64,384]{1,0:T(8,128)S(1)} %reshape.237) | copy-start | bytes 294916
  200.1 60.6 %reduce-scatter.15.cloned.1.call-start = ((), (), s32[]{:S(2)}) async-start(), calls=%async_computation.16 | async-start | bytes 245760 | tf_op jit(solution)/shard_map/while/body/eval_jaxpr/reduce_scatter | solution.py:176
  219.0 12.5 %copy-start.22 = (bf16[1,64,1536]{2,1,0:T(8,128)(2,1)S(1)}, bf16[1,64,1536]{2,1,0:T(8,128)(2,1)}, u32[]{:S(2)}) copy-start(bf16[1,64,1536]{2,1,0:T(8,128)(2,1)} %all-gather) | copy-start | bytes 589828
  220.0 42.3 %copy-start.36 = (f32[16]{0:T(128)}, f32[16]{0:T(128)S(1)}, u32[]{:S(2)}) copy-start(f32[16]{0:T(128)S(1)} %broadcast_multiply_fusion.7) | copy-start | bytes 196
  221.0 41.2 %copy-start.41 = (f32[16]{0:T(128)}, f32[16]{0:T(128)S(1)}, u32[]{:S(2)}) copy-start(f32[16]{0:T(128)S(1)} %add_rsqrt_fusion.1) | copy-start | bytes 196
  236.2 24.5 %copy-start.17 = (bf16[16,1536]{1,0:T(8,128)(2,1)S(1)}, bf16[16,1536]{1,0:T(8,128)(2,1)}, u32[]{:S(2)}) copy-start(bf16[16,1536]{1,0:T(8,128)(2,1)} %reduce-scatter.11.cloned.1.call-done) | copy-start | bytes 147460
  236.2 26.1 %copy-start.25 = (bf16[1,16,1536]{2,1,0:T(8,128)(2,1)S(1)}, bf16[1,16,1536]{2,1,0:T(8,128)(2,1)}, u32[]{:S(2)}) copy-start(bf16[1,16,1536]{2,1,0:T(8,128)(2,1)} %param.33) | copy-start | bytes 147460
  240.8 54.6 %copy-start.55 = (pred[2112]{0:T(1024)(128)(4,1)S(1)}, pred[2112]{0:T(1024)(128)(4,1)}, u32[]{:S(2)}) copy-start(pred[2112]{0:T(1024)(128)(4,1)} %copy-done.54) | copy-start | bytes 6340
  240.8 152.7 %all-gather.16.cloned.1.call-start = ((), (), s32[]{:S(2)}) async-start(), calls=%async_computation.17 | async-start | bytes 11796480 | tf_op jit(solution)/shard_map/all_gather | solution.py:86
  241.5 188.5 %reduce-scatter.19.cloned.1.call-start = ((), (), s32[]{:S(2)}) async-start(), calls=%async_computation.20 | async-start | bytes 1327104 | tf_op jit(solution)/shard_map/reduce_scatter | solution.py:318
  262.2 37.3 %copy-start.50 = (f32[16]{0:T(128)}, f32[16]{0:T(128)S(1)}, u32[]{:S(2)}) copy-start(f32[16]{0:T(128)S(1)} %get-tuple-element.159) | copy-start | bytes 196
  262.2 37.3 %copy-start.52 = (f32[16]{0:T(128)}, f32[16]{0:T(128)S(1)}, u32[]{:S(2)}) copy-start(f32[16]{0:T(128)S(1)} %get-tuple-element.160) | copy-start | bytes 196
  271.9 191.0 %reduce-scatter.17.cloned.1.call-start = ((), (), s32[]{:S(2)}) async-start(), calls=%async_computation.19 | async-start | bytes 1327104 | tf_op jit(solution)/shard_map/reduce_scatter | solution.py:309
  311.9 262.1 %all-reduce.11.cloned.1.call-start = ((), (), s32[]{:S(2)}) async-start(), calls=%async_computation.24 | async-start | bytes 4718592
  316.8 11.0 %copy-start.4 = (bf16[4,96,2112]{2,1,0:T(8,128)(2,1)}, bf16[4,96,2112]{2,1,0:T(8,128)(2,1)S(1)}, u32[]{:S(2)}) copy-start(bf16[4,96,2112]{2,1,0:T(8,128)(2,1)S(1)} %convolution_convert_fusion.3) | copy-start | bytes 4866052
  334.6 277.5 %all-gather.18.cloned.1.call-start = ((), (), s32[]{:S(2)}) async-start(), calls=%async_computation.18 | async-start | bytes 5898240 | tf_op jit(solution)/shard_map/all_gather | solution.py:85
  347.6 41.7 %all-to-all-start = ((bf16[2048,2,384]{2,1,0:T(2,128)(2,1)}), bf16[2048,2,384]{2,1,0:T(2,128)(2,1)}, u32[]{:S(2)}, u32[]{:S(2)}) async-start(bf16[2048,2,384]{2,1,0:T(2,128)(2,1)} %copy.126), calls=%async_computation.3 | async-start | bytes 6291456 | tf_op jit(solution)/shard_map/while/body/eval_jaxpr/all_to_all | solution.py:233
  352.3 307.3 %reduce-scatter.13.cloned.1.call-start = ((), (), s32[]{:S(2)}) async-start(), calls=%async_computation.15 | async-start | bytes 245760 | tf_op jit(solution)/shard_map/while/body/eval_jaxpr/reduce_scatter | solution.py:161
  357.0 378.5 %reduce-scatter.25.cloned.1.call-start = ((), (), s32[]{:S(2)}) async-start(), calls=%async_computation.23 | async-start | bytes 811008
  409.3 424.6 %reduce-scatter.21.cloned.1.call-start = ((), (), s32[]{:S(2)}) async-start(), calls=%async_computation.21 | async-start | bytes 5308416 | tf_op jit(solution)/shard_map/reduce_scatter | solution.py:303
  412.9 519.8 %reduce-scatter.23.cloned.1.call-start = ((), (), s32[]{:S(2)}) async-start(), calls=%async_computation.22 | async-start | bytes 5308416 | tf_op jit(solution)/shard_map/reduce_scatter | solution.py:306
  417.8 7.1 copy-start.56
  421.3 8.6 all-to-all-start.1
  576.0 36.2 %copy-start.40 = (f32[16]{0:T(128)S(1)}, f32[16]{0:T(128)}, u32[]{:S(2)}) copy-start(f32[16]{0:T(128)} %copy-done.39) | copy-start | bytes 196
  576.0 36.2 %copy-start.49 = (f32[16]{0:T(128)S(1)}, f32[16]{0:T(128)}, u32[]{:S(2)}) copy-start(f32[16]{0:T(128)} %copy-done.48) | copy-start | bytes 196
  582.2 33.7 %copy-start.31 = (f32[1536]{0:T(1024)S(1)}, f32[1536]{0:T(1024)}, u32[]{:S(2)}) copy-start(f32[1536]{0:T(1024)} %get-tuple-element.98) | copy-start | bytes 18436
  582.2 33.8 %copy-start.46 = (f32[1536]{0:T(1024)S(1)}, f32[1536]{0:T(1024)}, u32[]{:S(2)}) copy-start(f32[1536]{0:T(1024)} %get-tuple-element.87) | copy-start | bytes 18436
  582.2 33.8 %copy-start.47 = (f32[1536]{0:T(1024)S(1)}, f32[1536]{0:T(1024)}, u32[]{:S(2)}) copy-start(f32[1536]{0:T(1024)} %get-tuple-element.90) | copy-start | bytes 18436
  582.2 77.3 %copy-start.24 = (bf16[16,1536]{1,0:T(8,128)(2,1)S(1)}, bf16[16,1536]{1,0:T(8,128)(2,1)}, u32[]{:S(2)}) copy-start(bf16[16,1536]{1,0:T(8,128)(2,1)} %reduce-scatter.15.cloned.1.call-done) | copy-start | bytes 147460
  582.2 77.3 %copy-start.26 = (bf16[1,16,1536]{2,1,0:T(8,128)(2,1)S(1)}, bf16[1,16,1536]{2,1,0:T(8,128)(2,1)}, u32[]{:S(2)}) copy-start(bf16[1,16,1536]{2,1,0:T(8,128)(2,1)} %param.33) | copy-start | bytes 147460
  582.3 77.3 %copy-start.37 = (f32[16]{0:T(128)S(1)}, f32[16]{0:T(128)}, u32[]{:S(2)}) copy-start(f32[16]{0:T(128)} %copy-done.36) | copy-start | bytes 196
  582.3 77.3 %copy-start.42 = (f32[16]{0:T(128)S(1)}, f32[16]{0:T(128)}, u32[]{:S(2)}) copy-start(f32[16]{0:T(128)} %copy-done.41) | copy-start | bytes 196
  582.3 77.3 %copy-start.51 = (f32[16]{0:T(128)S(1)}, f32[16]{0:T(128)}, u32[]{:S(2)}) copy-start(f32[16]{0:T(128)} %copy-done.50) | copy-start | bytes 196
  582.3 77.3 %copy-start.53 = (f32[16]{0:T(128)S(1)}, f32[16]{0:T(128)}, u32[]{:S(2)}) copy-start(f32[16]{0:T(128)} %copy-done.52) | copy-start | bytes 196
  612.1 322.7 %copy-start.1 = (bf16[8,1536]{1,0:T(8,128)(2,1)S(1)}, bf16[8,1536]{1,0:T(8,128)(2,1)}, u32[]{:S(2)}) copy-start(bf16[8,1536]{1,0:T(8,128)(2,1)} %param.21) | copy-start | bytes 73732
  (28 other events, 75.4 us)
Sparse Core Ops, SparseCore 0:
  10.2 43.8 all-gather.11
  56.8 50.4 all-gather.9
  109.5 44.8 all-gather.7
  156.5 41.1 all-gather.13
  200.5 18.4 reduce-scatter.10
  240.9 19.7 reduce-scatter.14
  262.3 64.0 all-gather.15
  330.4 64.8 reduce-scatter.18
  399.2 63.7 reduce-scatter.16
  466.4 107.5 all-reduce.10
  575.6 36.5 all-gather.17
  614.4 19.8 reduce-scatter.12
  639.4 96.1 reduce-scatter.24
  739.1 94.7 reduce-scatter.20
  837.3 95.2 reduce-scatter.22
where the time goes:
time: 944 us; the launch traced here: 941 us
  waiting for transfers between devices  649 us (69%)
  matrix products  95.8 us (10%)
  blocking collectives  87.2 us (9%)
  local copies, waits for them, and re-layouts  54.7 us (6%)
  other arithmetic  28.2 us (3%)
  between operations  17.4 us (2%)
    unnamed x17, waiting for transfers between devices  187 us
    reduce_scatter x1, waiting for transfers between devices, body(): lax.psum_scatter(up_acc.astype(jnp.bfloat16), 'wide', scatter_dimension=0...  96.9 us
    reduce_scatter x1, waiting for transfers between devices, body(): lax.psum_scatter(down_acc.astype(jnp.bfloat16), 'wide', scatter_dimension...  96.6 us
    all_gather x1, waiting for transfers between devices, body(): lax.all_gather(keyval_weight, 'wide', axis=0, tiled=True)  51.6 us
    all_gather x1, waiting for transfers between devices, item_step(): lax.all_gather(media_nf.astype(jnp.bfloat16), 'narrow', axis=0, tiled=True)  42.8 us
    unnamed x1, blocking collectives  40.1 us
    all_to_all x1, waiting for transfers between devices, item_step(): lax.all_to_all(media_pairs, 'narrow', split_axis=0, concat_axis=2, tiled=...  31.9 us
    reduce_scatter x1, waiting for transfers between devices, body(): lax.psum_scatter(query_acc.astype(jnp.bfloat16), 'wide', scatter_dimensio...  31.3 us
  transfers between devices with their start and end apart: 17, of which 14 were waited for; matrix products, arithmetic and copies ran while one was open for 16% of the time, Pallas kernels for 0%

commit v1 on v0

v1 whole, which is shorter than its diff:
```python
import math

import jax
import jax.numpy as jnp
from jax import lax
from jax.sharding import PartitionSpec as P

HEADS = 16
HEAD_DIM = 96
FRAMES_MAX = 8
PATCHES = 256


EPS = 1e-05
ENT_COEF = 4.0
HIGH = lax.Precision.HIGHEST


def norm_forward(values, norm_gain, norm_bias):
    row_mean = jnp.mean(values, axis=-1, keepdims=True)
    centered = values - row_mean
    inv_std = lax.rsqrt(jnp.mean(centered * centered, axis=-1, keepdims=True) + EPS)
    normed = centered * inv_std
    return (normed * norm_gain + norm_bias, normed, inv_std)


def norm_backward(grad_out, normed, inv_std, norm_gain):
    scaled = grad_out * norm_gain
    grad_in = inv_std * (
        scaled
        - jnp.mean(scaled, axis=-1, keepdims=True)
        - normed * jnp.mean(scaled * normed, axis=-1, keepdims=True)
    )
    return (grad_in, jnp.sum(grad_out * normed, axis=0), jnp.sum(grad_out, axis=0))


def gelu_slope(pre_act):
    cdf_part = 0.5 * (1.0 + lax.erf(pre_act * (1.0 / math.sqrt(2.0))))
    density = jnp.exp(-0.5 * pre_act * pre_act) * (1.0 / math.sqrt(2.0 * math.pi))
    return cdf_part + pre_act * density


def body(
    media_feats,
    latents,
    frame_counts,
    media_mask,
    time_embed,
    media_gain,
    media_bias,
    latent_gain,
    latent_bias,
    ffn_gain,
    ffn_bias,
    query_weight,
    keyval_weight,
    output_weight,
    up_weight,
    down_weight,
    cotangent,
):
    width = media_feats.shape[2]
    own_media = media_feats.shape[1]
    own_latent = latents.shape[1]
    narrow_size = lax.axis_size("narrow")
    wide_size = lax.axis_size("wide")
    narrow_pos = lax.axis_index("narrow")
    media_total = own_media * narrow_size
    latent_total = own_latent * narrow_size
    head_local = HEADS // narrow_size
    cols = head_local * HEAD_DIM
    key_total = media_total + latent_total
    f32, bf16 = jnp.float32, jnp.bfloat16

    def mm(spec, a, b):
        return jnp.einsum(spec, a, b, preferred_element_type=f32)

    all_ids = jnp.arange(media_total, dtype=jnp.int32) // PATCHES
    valid_one = (all_ids < frame_counts[0]) & (media_mask[0] > 0)
    local_count = jnp.sum(valid_one.astype(f32)) + float(latent_total)
    total_count = lax.psum(local_count, "wide")
    ent_weight = ENT_COEF * float(wide_size * media_total) / total_count
    kv_own = lax.all_gather(keyval_weight, "wide", axis=0, tiled=True).reshape(width, 2 * cols)
    query_own = lax.all_gather(query_weight, "wide", axis=0, tiled=True)
    output_own = lax.all_gather(output_weight, "wide", axis=1, tiled=True)
    own_ids = (narrow_pos * own_media + jnp.arange(own_media, dtype=jnp.int32)) // PATCHES
    frame_onehot = own_ids[:, None] == jnp.arange(FRAMES_MAX, dtype=jnp.int32)[None, :]
    time_rows = jnp.dot(frame_onehot.astype(bf16), time_embed, preferred_element_type=f32)
    score_scale = HEAD_DIM ** (-0.5)
    media_one, latent_one, cot_one = media_feats[0], latents[0], cotangent[0]
    media_nf, media_hat, media_istd = norm_forward(
        media_one.astype(f32) + time_rows, media_gain, media_bias
    )
    latent_f32 = latent_one.astype(f32)
    latent_nf, latent_hat, latent_istd = norm_forward(latent_f32, latent_gain, latent_bias)
    latent_all = lax.all_gather(latent_nf.astype(bf16), "narrow", axis=0, tiled=True)
    cot_all = lax.all_gather(cot_one, "narrow", axis=0, tiled=True)
    media_all = lax.all_gather(media_nf.astype(bf16), "narrow", axis=0, tiled=True)
    keys_in = jnp.concatenate([media_all, latent_all], axis=0)
    query_act = mm("ld,dc->lc", latent_all, query_own).astype(bf16)
    key_vals = mm("kd,dc->kc", keys_in, kv_own).astype(bf16)
    query_heads = query_act.reshape(latent_total, head_local, HEAD_DIM)
    key_heads = key_vals[:, :cols].reshape(key_total, head_local, HEAD_DIM)
    value_heads = key_vals[:, cols:].reshape(key_total, head_local, HEAD_DIM)
    key_valid = jnp.concatenate([valid_one, jnp.ones((latent_total,), dtype=bool)])
    scores = mm("lhd,khd->hlk", query_heads, key_heads) * score_scale
    open_keys = key_valid[None, None, :]
    masked = jnp.where(open_keys, scores, -1e30)
    row_top = jnp.max(masked, axis=-1)
    expo = jnp.exp(masked - row_top[..., None])
    prob_all = expo / jnp.sum(expo, axis=-1)[..., None]
    prob_low = prob_all.astype(bf16)
    plain_scores = jnp.where(open_keys, scores, 0.0)
    mean_score = jnp.sum(prob_all * plain_scores, axis=-1)
    attn_out = mm("hlk,khd->lhd", prob_low, value_heads).reshape(latent_total, cols)
    attn_low = attn_out.astype(bf16)
    branch_part = mm("lc,cd->ld", attn_low, output_own)
    branch_own = lax.psum_scatter(
        branch_part.astype(bf16), "narrow", scatter_dimension=0, tiled=True
    ).astype(f32)
    latent_mid = latent_f32 + branch_own
    hidden_f, hidden_hat, hidden_istd = norm_forward(latent_mid, ffn_gain, ffn_bias)
    hidden_all = lax.all_gather(hidden_f.astype(bf16), "narrow", axis=0, tiled=True)
    pre_act = mm("ld,df->lf", hidden_all, up_weight)
    act_low = jax.nn.gelu(pre_act, approximate=False).astype(bf16)
    grad_act = mm("ld,fd->lf", cot_all, down_weight)
    grad_pre = (grad_act * gelu_slope(pre_act)).astype(bf16)
    hidden_part = mm("lf,df->ld", grad_pre, up_weight)
    grad_hidden = lax.psum_scatter(
        hidden_part.astype(bf16), "narrow", scatter_dimension=0, tiled=True
    ).astype(f32)
    grad_norm, fg_part, fb_part = norm_backward(grad_hidden, hidden_hat, hidden_istd, ffn_gain)
    grad_mid = cot_one.astype(f32) + grad_norm
    grad_branch_all = lax.all_gather(grad_mid.astype(bf16), "narrow", axis=0, tiled=True)
    ffn_part = mm("lf,fd->ld", act_low, down_weight)
    ffn_own = lax.psum_scatter(
        ffn_part.astype(bf16), "narrow", scatter_dimension=0, tiled=True
    ).astype(f32)
    out_one = (latent_mid + ffn_own).astype(bf16)
    grad_attn = mm("ld,cd->lc", grad_branch_all, output_own).astype(bf16)
    row_dots = jnp.sum(
        (grad_attn.astype(f32) * attn_out).reshape(latent_total, head_local, HEAD_DIM), axis=-1
    )
    shift_rows = (jnp.transpose(row_dots, (1, 0)) - ent_weight * mean_score)[..., None]
    grad_heads = grad_attn.reshape(latent_total, head_local, HEAD_DIM)
    grad_prob = mm("lhd,khd->hlk", grad_heads, value_heads)
    grad_scores = (prob_all * (grad_prob - ent_weight * plain_scores - shift_rows)).astype(bf16)
    grad_values = mm("hlk,lhd->khd", prob_low, grad_heads).reshape(key_total, cols)
    grad_keys = mm("hlk,lhd->khd", grad_scores, query_heads).reshape(key_total, cols) * score_scale
    grad_query = (
        mm("hlk,khd->lhd", grad_scores, key_heads).reshape(latent_total, cols) * score_scale
    ).astype(bf16)
    grad_pairs = jnp.concatenate([grad_keys, grad_values], axis=-1).astype(bf16)
    rows_part = mm("ke,de->kd", grad_pairs, kv_own)
    grad_media_rows = lax.psum_scatter(
        rows_part[:media_total].astype(bf16), "narrow", scatter_dimension=0, tiled=True
    ).astype(f32)
    latent_part = rows_part[media_total:] + mm("lc,dc->ld", grad_query, query_own)
    grad_latent_normed = lax.psum_scatter(
        latent_part.astype(bf16), "narrow", scatter_dimension=0, tiled=True
    ).astype(f32)
    keyval_grad = mm("kd,ke->de", keys_in, grad_pairs)
    keyval_sum = lax.psum_scatter(
        keyval_grad.astype(bf16), "wide", scatter_dimension=0, tiled=True
    ).astype(f32).reshape(width // wide_size, 2, cols)
    tall = lax.all_gather(
        jnp.concatenate([act_low, grad_pre, attn_low, grad_query], axis=1), "wide", axis=0, tiled=True
    )
    ff = up_weight.shape[1]
    act_g, pre_g, attn_g, query_g = (
        tall[:, :ff], tall[:, ff : 2 * ff], tall[:, 2 * ff : 2 * ff + cols], tall[:, 2 * ff + cols :]
    )
    cut = jnp.stack([latent_all, cot_all, hidden_all, grad_branch_all], axis=0)
    cut = cut.reshape(4, latent_total, wide_size, width // wide_size).transpose(2, 0, 1, 3)
    cut = lax.all_to_all(cut, "wide", split_axis=0, concat_axis=0, tiled=True)
    cut = cut.transpose(1, 0, 2, 3).reshape(4, wide_size * latent_total, width // wide_size)
    up_sum = mm("rd,rf->df", cut[2], pre_g)
    down_sum = mm("rf,rd->fd", act_g, cut[1])
    output_sum = mm("rc,rd->cd", attn_g, cut[3])
    query_sum = mm("rd,rc->dc", cut[0], query_g)
    grad_media_in, mg_part, mb_part = norm_backward(
        grad_media_rows, media_hat, media_istd, media_gain
    )
    time_part = jnp.einsum(
        "mf,md->fd", frame_onehot.astype(f32), grad_media_in, precision=HIGH
    )
    grad_latent_in, lg_part, lb_part = norm_backward(
        grad_latent_normed, latent_hat, latent_istd, latent_gain
    )
    grad_latent_one = (grad_mid + grad_latent_in).astype(bf16)
    vectors = jnp.concatenate(
        [time_part, jnp.stack([mg_part, mb_part, lg_part, lb_part, fg_part, fb_part])], axis=0
    )
    vec = lax.psum_scatter(vectors, ("wide", "narrow"), scatter_dimension=1, tiled=True)
    return (
        out_one[None],
        grad_media_in.astype(bf16)[None],
        grad_latent_one[None],
        vec[:FRAMES_MAX],
        vec[FRAMES_MAX],
        vec[FRAMES_MAX + 1],
        vec[FRAMES_MAX + 2],
        vec[FRAMES_MAX + 3],
        vec[FRAMES_MAX + 4],
        vec[FRAMES_MAX + 5],
        query_sum,
        keyval_sum,
        output_sum,
        up_sum,
        down_sum,
    )


def solution(mesh):
    placed = (
        P("wide", "narrow", None),
        P("wide", "narrow", None),
        P("wide"),
        P("wide", None),
        P(),
        P(),
        P(),
        P(),
        P(),
        P(),
        P(),
        P("wide", "narrow"),
        P("wide", None, "narrow"),
        P("narrow", "wide"),
        P(None, "narrow"),
        P("narrow", None),
        P("wide", "narrow", None),
    )
    return jax.shard_map(
        body,
        mesh=mesh,
        in_specs=placed,
        out_specs=(
            P("wide", "narrow", None),
            P("wide", "narrow", None),
            P("wide", "narrow", None),
            P(None, ("wide", "narrow")),
            P(("wide", "narrow")),
            P(("wide", "narrow")),
            P(("wide", "narrow")),
            P(("wide", "narrow")),
            P(("wide", "narrow")),
            P(("wide", "narrow")),
            P("wide", "narrow"),
            P("wide", None, "narrow"),
            P("narrow", "wide"),
            P("wide", "narrow"),
            P("narrow", "wide"),
        ),
        check_vma=False,
    )
```

time: 944 us -> 679 us (0.72)
  waiting for transfers between devices: 649 us -> 449 us
  blocking collectives: 87.2 us -> 44.8 us
  matrix products: 95.8 us -> 79.9 us
    reduce_scatter x7 -> x6, waiting for transfers between devices: 256 us -> 108 us  [the longest x1 52.1 us: body(): lax.psum_scatter(rows_part[:media_total].astype(bf16), 'narrow', scatter_...]
    unnamed x17 -> x13, waiting for transfers between devices: 187 us -> 96.5 us
    unnamed x1 -> x0, blocking collectives: 40.1 us -> none
    all_gather x5 -> x4, waiting for transfers between devices: 119 us -> 159 us  [the longest x1 69.3 us: body(): lax.all_gather(jnp.concatenate([act_low, grad_pre, attn_low, grad_query],...]
    dot_general x23, matrix products: 88.5 us -> 76.3 us  [the longest x21 73 us: mm(): return jnp.einsum(spec, a, b, preferred_element_type=f32)]
    slice x3 -> x6, local copies, waits for them, and re-layouts: 9.58 us -> 20.7 us  [the longest x1 7.99 us: body(): rows_part[:media_total].astype(bf16)]
    unnamed x128 -> x122, local copies, waits for them, and re-layouts: 15.5 us -> 21.7 us
    all_to_all x2 -> x1, waiting for transfers between devices: 35.7 us -> 33.9 us  [body(): cut = lax.all_to_all(cut, 'wide', split_axis=0, concat_axis=0, tiled=True)]
  transfers between devices with their start and end apart: 17 -> 13, of which waited for: 14 -> 11; matrix products, arithmetic and copies ran while one was open for 16% -> 14% of each run, Pallas kernels for 0% -> 0%
where the time goes in v1:
time: 679 us; the launch traced here: 677 us
  waiting for transfers between devices  449 us (66%)
  matrix products  79.9 us (12%)
  local copies, waits for them, and re-layouts  58.9 us (9%)
  blocking collectives  44.8 us (7%)
  other arithmetic  21.2 us (3%)
  between operations  16.9 us (2%)
    unnamed x13, waiting for transfers between devices  96.5 us
    dot_general x21, matrix products, mm(): return jnp.einsum(spec, a, b, preferred_element_type=f32)  73 us
    all_gather x1, waiting for transfers between devices, body(): lax.all_gather(jnp.concatenate([act_low, grad_pre, attn_low, grad_query],...  69.3 us
    reduce_scatter x1, waiting for transfers between devices, body(): lax.psum_scatter(rows_part[:media_total].astype(bf16), 'narrow', scatter_...  52.1 us
    all_gather x1, waiting for transfers between devices, body(): lax.all_gather(keyval_weight, 'wide', axis=0, tiled=True)  51 us
    reduce_scatter x1, waiting for transfers between devices, body(): lax.psum_scatter(keyval_grad.astype(bf16), 'wide', scatter_dimension=0, t...  43.5 us
    all_gather x1, waiting for transfers between devices, body(): lax.all_gather(media_nf.astype(bf16), 'narrow', axis=0, tiled=True)  43.4 us
    all_to_all x1, waiting for transfers between devices, body(): cut = lax.all_to_all(cut, 'wide', split_axis=0, concat_axis=0, tiled=True)  33.9 us
  transfers between devices with their start and end apart: 13, of which 11 were waited for; matrix products, arithmetic and copies ran while one was open for 14% of the time, Pallas kernels for 0%

profile of v1, /device:TPU:0, one launch (start us, length us, event | category | flops | bytes accessed | tf_op | source)
XLA Modules:
  0.0 676.7 jit_solution(7399036223634174720)
XLA Ops:
  8.8 2.1 fusion.103
  15.6 6.9 %all_gather.28 = bf16[64,1536]{1,0:T(8,128)(2,1)S(1)} all-gather(bf16[16,1536]{1,0:T(8,128)(2,1)S(1)} %fusion.63), channel_id=1, replica_groups=mesh['wide'=8,'narrow'=4] {'narrow'}, dimensions={0}, use_global_device_ids=true | all-gather | bytes 245760 | tf_op jit(solution)/shard_map/all_gather | solution.py:96
  23.1 31.0 %all-gather.11.cloned.1.call-done = bf16[1536,384]{1,0:T(8,128)(2,1)} async-done(((bf16[192,384]{1,0:T(8,128)(2,1)}), bf16[1536,384]{1,0:T(8,128)(2,1)}) %all-gather.11.cloned.1.call-update) | async-done | bytes 1179664 | tf_op jit(solution)/shard_map/all_gather | solution.py:84
  55.8 51.0 %all-gather.9.cloned.1.call-done = bf16[1536,2,384]{2,1,0:T(2,128)(2,1)} async-done(((bf16[192,2,384]{2,1,0:T(2,128)(2,1)}), bf16[1536,2,384]{2,1,0:T(2,128)(2,1)}) %all-gather.9.cloned.1.call-update) | async-done | bytes 2359312 | tf_op jit(solution)/shard_map/all_gather | solution.py:83
  106.8 3.6 copy.106
  110.4 43.4 %all-gather.7.cloned.1.call-done = bf16[2048,1536]{1,0:T(8,128)(2,1)} async-done(((bf16[512,1536]{1,0:T(8,128)(2,1)}), bf16[2048,1536]{1,0:T(8,128)(2,1)}) %all-gather.7.cloned.1.call-update) | async-done | bytes 6291472 | tf_op jit(solution)/shard_map/all_gather | solution.py:98
  153.8 3.3 constant_dynamic-update-slice_fusion.1
  157.3 5.4 convolution_convert_fusion
  162.7 2.1 fusion.100
  164.8 3.8 copy.88
  168.6 3.8 copy.87
  172.3 3.7 fusion.104
  176.0 2.9 convolution_bitcast_fusion
  181.4 15.6 %all-gather.13.cloned.1.call-done = bf16[384,1536]{0,1:T(8,128)(2,1)} async-done(((bf16[384,192]{0,1:T(8,128)(2,1)}), bf16[384,1536]{0,1:T(8,128)(2,1)}) %all-gather.13.cloned.1.call-update) | async-done | bytes 1179664 | tf_op jit(solution)/shard_map/all_gather | solution.py:85
  197.0 2.5 convolution_convert_fusion.5
  200.2 19.6 %psum.7 = f32[]{:T(128)} all-reduce(f32[]{:T(128)S(6)} %add.128), channel_id=1, replica_groups=mesh['wide'=8,'narrow'=4] {'wide'}, use_global_device_ids=true, to_apply=%region_14.15 | all-reduce | flops 1 | bytes 8 | tf_op jit(solution)/shard_map/psum | solution.py:81
  220.5 7.1 %all-gather = bf16[1,64,1536]{2,1,0:T(8,128)(2,1)} all-gather(bf16[1,16,1536]{2,1,0:T(8,128)(2,1)} %param.33), channel_id=2, replica_groups=mesh['wide'=8,'narrow'=4] {'narrow'}, dimensions={1}, use_global_device_ids=true | all-gather | bytes 245760 | tf_op jit(solution)/shard_map/all_gather | solution.py:97
  230.5 5.6 all_gather.32
  236.1 4.7 fusion.30
  240.8 3.9 fusion.14
  245.4 4.6 convolution_convert_fusion.3
  250.2 4.7 multiply_reduce_fusion.1
  254.9 11.4 %reduce-scatter.14.cloned.1.call-done = bf16[16,1536]{1,0:T(8,128)(2,1)} async-done(((bf16[64,1536]{1,0:T(8,128)(2,1)}), bf16[16,1536]{1,0:T(8,128)(2,1)}) %reduce-scatter.14.cloned.1.call-update) | async-done | bytes 49168 | tf_op jit(solution)/shard_map/reduce_scatter | solution.py:129
  268.7 5.6 all_gather.34
  275.0 2.2 convert_multiply_fusion.6
  281.4 3.6 convolution_convert_fusion.1
  290.9 8.3 %fusion.16 = f32[2112,1536]{1,0:T(8,128)S(1)} fusion(bf16[1536,768]{1,0:T(8,128)(2,1)} %bitcast.147, bf16[2112,384]{0,1:T(8,128)(2,1)} %bitcast.166, bf16[2112,384]{0,1:T(8,128)(2,1)} %bitcast.152), kind=kOutput, calls=%fused_computation.37 | convolution fusion | flops 4989321216 | bytes 18579456 | tf_op jit(solution)/shard_map/ke,de->kd/dot_general | solution.py:76
  299.3 4.6 copy-done.7
  305.1 4.1 convolution_convert_fusion.4
  309.5 10.1 %convolution_convert_fusion.2 = bf16[1536,768]{1,0:T(8,128)(2,1)} fusion(bf16[2112,1536]{1,0:T(8,128)(2,1)} %copy-done.4, bf16[2112,384]{0,1:T(8,128)(2,1)} %bitcast.167, bf16[2112,384]{0,1:T(8,128)(2,1)} %bitcast.153), kind=kOutput, calls=%fused_computation.19 | convolution fusion | flops 4990500864 | bytes 12091392 | tf_op jit(solution)/shard_map/kd,ke->de/dot_general | solution.py:76
  322.3 8.0 %slice.110 = bf16[2048,1536]{1,0:T(8,128)(2,1)} slice(f32[2112,1536]{1,0:T(8,128)} %copy-done.7), slice={[0:2048], [0:1536]} | slice | bytes 12582912 | tf_op jit(solution)/shard_map/slice | solution.py:156
  330.3 1.9 stack.40
  333.1 1.9 stack.41
  335.0 1.9 stack.42
  339.6 5.5 all-to-all-start
  348.9 33.9 %all-to-all-done = bf16[8,4,64,192]{3,2,1,0:T(8,128)(2,1)} async-done(((bf16[8,4,64,192]{3,2,1,0:T(8,128)(2,1)}), bf16[8,4,64,192]{3,2,1,0:T(8,128)(2,1)}, u32[]{:S(2)}, u32[]{:S(2)}) %all-to-all-start) | async-done | bytes 786464 | tf_op jit(solution)/shard_map/all_to_all | solution.py:175
  382.8 2.1 fusion.101
  384.9 43.5 %reduce-scatter.20.cloned.1.call-done = bf16[192,768]{1,0:T(8,128)(2,1)} async-done(((bf16[1536,768]{1,0:T(8,128)(2,1)}), bf16[192,768]{1,0:T(8,128)(2,1)}) %reduce-scatter.20.cloned.1.call-update) | async-done | bytes 294928 | tf_op jit(solution)/shard_map/reduce_scatter | solution.py:163
  428.4 2.1 reshape.193
  430.5 69.3 %all-gather.15.cloned.1.call-done = bf16[512,3840]{1,0:T(8,128)(2,1)} async-done(((bf16[64,3840]{1,0:T(8,128)(2,1)}), bf16[512,3840]{1,0:T(8,128)(2,1)}) %all-gather.15.cloned.1.call-update) | async-done | bytes 3932176 | tf_op jit(solution)/shard_map/all_gather | solution.py:166
  499.7 2.1 fusion.35
  501.8 3.0 fusion.18
  504.8 3.0 fusion.20
  507.8 52.1 %reduce-scatter.16.cloned.1.call-done = bf16[512,1536]{1,0:T(8,128)(2,1)} async-done(((bf16[2048,1536]{1,0:T(8,128)(2,1)}), bf16[512,1536]{1,0:T(8,128)(2,1)}) %reduce-scatter.16.cloned.1.call-update) | async-done | bytes 1572880 | tf_op jit(solution)/shard_map/reduce_scatter | solution.py:155
  559.8 2.9 fusion.13
  562.8 2.1 convert_bitcast_fusion
  567.5 2.0 fusion.37
  569.5 94.4 %reduce-scatter.22.cloned.1.call-done = f32[48,14]{1,0:T(8,128)} async-done(((f32[1536,14]{1,0:T(8,128)}), f32[48,14]{1,0:T(8,128)}) %reduce-scatter.22.cloned.1.call-update) | async-done | bytes 2704
  (203 shorter events, 47.1 us)
Async XLA Ops:
  7.2 46.9 %all-gather.11.cloned.1.call-start = ((), (), s32[]{:S(2)}) async-start(), calls=%async_computation.10 | async-start | bytes 1327104 | tf_op jit(solution)/shard_map/all_gather | solution.py:84
  7.9 98.9 %all-gather.9.cloned.1.call-start = ((), (), s32[]{:S(2)}) async-start(), calls=%async_computation.9 | async-start | bytes 2654208 | tf_op jit(solution)/shard_map/all_gather | solution.py:83
  8.7 145.2 %all-gather.7.cloned.1.call-start = ((), (), s32[]{:S(2)}) async-start(), calls=%async_computation.8 | async-start | bytes 7864320 | tf_op jit(solution)/shard_map/all_gather | solution.py:98
  11.6 3.9 copy-start.26
  11.6 3.9 copy-start.39
  13.4 183.7 %all-gather.13.cloned.1.call-start = ((), (), s32[]{:S(2)}) async-start(), calls=%async_computation.11 | async-start | bytes 1327104 | tf_op jit(solution)/shard_map/all_gather | solution.py:85
  13.9 213.7 %reduce-scatter.10.cloned.1.call-start = ((), (), s32[]{:S(2)}) async-start(), calls=%async_computation.12 | async-start | bytes 245760 | tf_op jit(solution)/shard_map/reduce_scatter | solution.py:118
  14.8 95.6 %copy-start.35 = (f32[16]{0:T(128)}, f32[16]{0:T(128)S(1)}, u32[]{:S(2)}) copy-start(f32[16]{0:T(128)S(1)} %broadcast_multiply_fusion.8) | copy-start | bytes 196
  23.1 227.1 %copy-start.49 = (pred[2112]{0:T(1024)(128)(4,1)}, pred[2112]{0:T(1024)(128)(4,1)S(1)}, u32[]{:S(2)}) copy-start(pred[2112]{0:T(1024)(128)(4,1)S(1)} %concatenate.18) | copy-start | bytes 6340
  55.8 116.6 %copy-start.22 = (bf16[64,4,96]{2,1,0:T(4,128)(2,1)}, bf16[64,4,96]{2,1,0:T(4,128)(2,1)S(1)}, u32[]{:S(2)}) copy-start(bf16[64,4,96]{2,1,0:T(4,128)(2,1)S(1)} %reshape.183) | copy-start | bytes 147460
  157.2 5.5 copy-start.4
  176.0 74.2 %copy-start.54 = (f32[4,64]{1,0:T(4,128)}, f32[4,64]{1,0:T(4,128)S(1)}, u32[]{:S(2)}) copy-start(f32[4,64]{1,0:T(4,128)S(1)} %get-tuple-element.47) | copy-start | bytes 3076
  179.0 50.6 %copy-start.24 = (f32[1536]{0:T(1024)S(1)}, f32[1536]{0:T(1024)}, u32[]{:S(2)}) copy-start(f32[1536]{0:T(1024)} %param.26) | copy-start | bytes 18436
  179.0 50.6 %copy-start.40 = (f32[1536]{0:T(1024)S(1)}, f32[1536]{0:T(1024)}, u32[]{:S(2)}) copy-start(f32[1536]{0:T(1024)} %param.27) | copy-start | bytes 18436
  180.8 60.0 %copy-start.15 = (f32[64,384]{1,0:T(8,128)}, f32[64,384]{1,0:T(8,128)S(1)}, u32[]{:S(2)}) copy-start(f32[64,384]{1,0:T(8,128)S(1)} %reshape.185) | copy-start | bytes 294916
  199.5 66.8 %reduce-scatter.14.cloned.1.call-start = ((), (), s32[]{:S(2)}) async-start(), calls=%async_computation.14 | async-start | bytes 245760 | tf_op jit(solution)/shard_map/reduce_scatter | solution.py:129
  228.6 39.2 %copy-start.32 = (f32[16]{0:T(128)}, f32[16]{0:T(128)S(1)}, u32[]{:S(2)}) copy-start(f32[16]{0:T(128)S(1)} %broadcast_multiply_fusion.7) | copy-start | bytes 196
  229.6 38.2 %copy-start.37 = (f32[16]{0:T(128)}, f32[16]{0:T(128)S(1)}, u32[]{:S(2)}) copy-start(f32[16]{0:T(128)S(1)} %add_rsqrt_fusion.1) | copy-start | bytes 196
  236.1 4.7 copy-start.16
  236.1 4.7 copy-start.10
  250.0 16.3 %copy-start.12 = (bf16[16,1536]{1,0:T(8,128)(2,1)S(1)}, bf16[16,1536]{1,0:T(8,128)(2,1)}, u32[]{:S(2)}) copy-start(bf16[16,1536]{1,0:T(8,128)(2,1)} %reduce-scatter.10.cloned.1.call-done) | copy-start | bytes 147460
  250.0 17.9 %copy-start.19 = (bf16[1,16,1536]{2,1,0:T(8,128)(2,1)S(1)}, bf16[1,16,1536]{2,1,0:T(8,128)(2,1)}, u32[]{:S(2)}) copy-start(bf16[1,16,1536]{2,1,0:T(8,128)(2,1)} %param.33) | copy-start | bytes 147460
  250.0 95.3 %reduce-scatter.18.cloned.1.call-start = ((), (), s32[]{:S(2)}) async-start(), calls=%async_computation.16 | async-start | bytes 245760 | tf_op jit(solution)/shard_map/reduce_scatter | solution.py:159
  267.8 9.5 %copy-start.45 = (f32[16]{0:T(128)}, f32[16]{0:T(128)S(1)}, u32[]{:S(2)}) copy-start(f32[16]{0:T(128)S(1)} %get-tuple-element.55) | copy-start | bytes 196
  267.8 9.5 %copy-start.47 = (f32[16]{0:T(128)}, f32[16]{0:T(128)S(1)}, u32[]{:S(2)}) copy-start(f32[16]{0:T(128)S(1)} %get-tuple-element.56) | copy-start | bytes 196
  281.4 3.7 copy-start.50
  281.4 3.7 copy-start.53
  281.4 3.7 copy-start.55
  290.9 8.4 %copy-start.21 = (bf16[64,384]{1,0:T(8,128)(2,1)}, bf16[64,384]{1,0:T(8,128)(2,1)S(1)}, u32[]{:S(2)}) copy-start(bf16[64,384]{1,0:T(8,128)(2,1)S(1)} %convert_element_type.140) | copy-start | bytes 147460
  290.9 13.0 %copy-start.6 = (bf16[1536,384]{1,0:T(8,128)(2,1)S(1)}, bf16[1536,384]{1,0:T(8,128)(2,1)}, u32[]{:S(2)}) copy-start(bf16[1536,384]{1,0:T(8,128)(2,1)} %all-gather.11.cloned.1.call-done) | copy-start | bytes 3538948
  299.3 4.6 copy-start.7
  305.1 42.2 %reduce-scatter.12.cloned.1.call-start = ((), (), s32[]{:S(2)}) async-start(), calls=%async_computation.13 | async-start | bytes 245760 | tf_op jit(solution)/shard_map/reduce_scatter | solution.py:136
  309.2 119.2 %reduce-scatter.20.cloned.1.call-start = ((), (), s32[]{:S(2)}) async-start(), calls=%async_computation.18 | async-start | bytes 2654208 | tf_op jit(solution)/shard_map/reduce_scatter | solution.py:163
  319.6 180.1 %all-gather.15.cloned.1.call-start = ((), (), s32[]{:S(2)}) async-start(), calls=%async_computation.17 | async-start | bytes 4423680 | tf_op jit(solution)/shard_map/all_gather | solution.py:166
  322.3 237.5 %reduce-scatter.16.cloned.1.call-start = ((), (), s32[]{:S(2)}) async-start(), calls=%async_computation.15 | async-start | bytes 7864320 | tf_op jit(solution)/shard_map/reduce_scatter | solution.py:155
  338.3 6.9 %copy-start.29 = (f32[1536]{0:T(1024)S(1)}, f32[1536]{0:T(1024)}, u32[]{:S(2)}) copy-start(f32[1536]{0:T(1024)} %get-tuple-element.19) | copy-start | bytes 18436
  338.3 6.9 %copy-start.28 = (f32[1536]{0:T(1024)S(1)}, f32[1536]{0:T(1024)}, u32[]{:S(2)}) copy-start(f32[1536]{0:T(1024)} %get-tuple-element.25) | copy-start | bytes 18436
  338.3 7.0 %copy-start.36 = (f32[16]{0:T(128)S(1)}, f32[16]{0:T(128)}, u32[]{:S(2)}) copy-start(f32[16]{0:T(128)} %copy-done.35) | copy-start | bytes 196
  338.4 7.0 %copy-start.44 = (f32[16]{0:T(128)S(1)}, f32[16]{0:T(128)}, u32[]{:S(2)}) copy-start(f32[16]{0:T(128)} %copy-done.43) | copy-start | bytes 196
  338.4 8.9 %copy-start.18 = (bf16[16,1536]{1,0:T(8,128)(2,1)S(1)}, bf16[16,1536]{1,0:T(8,128)(2,1)}, u32[]{:S(2)}) copy-start(bf16[16,1536]{1,0:T(8,128)(2,1)} %reduce-scatter.14.cloned.1.call-done) | copy-start | bytes 147460
  338.4 8.9 %copy-start.20 = (bf16[1,16,1536]{2,1,0:T(8,128)(2,1)S(1)}, bf16[1,16,1536]{2,1,0:T(8,128)(2,1)}, u32[]{:S(2)}) copy-start(bf16[1,16,1536]{2,1,0:T(8,128)(2,1)} %param.33) | copy-start | bytes 147460
  338.4 8.9 %copy-start.33 = (f32[16]{0:T(128)S(1)}, f32[16]{0:T(128)}, u32[]{:S(2)}) copy-start(f32[16]{0:T(128)} %copy-done.32) | copy-start | bytes 196
  338.4 8.9 %copy-start.38 = (f32[16]{0:T(128)S(1)}, f32[16]{0:T(128)}, u32[]{:S(2)}) copy-start(f32[16]{0:T(128)} %copy-done.37) | copy-start | bytes 196
  338.4 8.9 %copy-start.46 = (f32[16]{0:T(128)S(1)}, f32[16]{0:T(128)}, u32[]{:S(2)}) copy-start(f32[16]{0:T(128)} %copy-done.45) | copy-start | bytes 196
  338.4 8.9 %copy-start.48 = (f32[16]{0:T(128)S(1)}, f32[16]{0:T(128)}, u32[]{:S(2)}) copy-start(f32[16]{0:T(128)} %copy-done.47) | copy-start | bytes 196
  339.6 43.1 %all-to-all-start = ((bf16[8,4,64,192]{3,2,1,0:T(8,128)(2,1)}), bf16[8,4,64,192]{3,2,1,0:T(8,128)(2,1)}, u32[]{:S(2)}, u32[]{:S(2)}) async-start(bf16[8,4,64,192]{3,2,1,0:T(8,128)(2,1)} %copy.96), calls=%async_computation.5 | async-start | bytes 2097152 | tf_op jit(solution)/shard_map/all_to_all | solution.py:175
  345.2 318.7 %reduce-scatter.22.cloned.1.call-start = ((), (), s32[]{:S(2)}) async-start(), calls=%async_computation.19 | async-start | bytes 811008
  565.0 104.9 %copy-start.1 = (bf16[8,1536]{1,0:T(8,128)(2,1)S(1)}, bf16[8,1536]{1,0:T(8,128)(2,1)}, u32[]{:S(2)}) copy-start(bf16[8,1536]{1,0:T(8,128)(2,1)} %param.21) | copy-start | bytes 73732
  (21 other events, 45.9 us)
Sparse Core Ops, SparseCore 0:
  10.2 43.8 all-gather.10
  56.2 50.4 all-gather.8
  108.9 44.8 all-gather.6
  155.9 41.1 all-gather.12
  199.9 18.4 reduce-scatter.9
  250.1 16.1 reduce-scatter.13
  305.2 19.7 reduce-scatter.17
  327.5 19.7 reduce-scatter.11
  350.8 77.5 reduce-scatter.19
  431.0 68.6 all-gather.14
  502.3 57.4 reduce-scatter.15
  567.6 96.2 reduce-scatter.21

commit v2 on v1

v2 whole, which is shorter than its diff:
```python
import functools
import math

import jax
import jax.numpy as jnp
from jax import lax
from jax.experimental import pallas as pl
from jax.experimental.pallas import tpu as pltpu
from jax.sharding import PartitionSpec as P

HEADS = 16
HEAD_DIM = 96
FRAMES_MAX = 8
PATCHES = 256
EPS = 1e-05
ENT_COEF = 4.0
NEG = -1e30
LANES = 128
MESH = pl.DeviceIdType.MESH
F32 = jnp.float32
BF16 = jnp.bfloat16


def nn(a, b):
    return lax.dot_general(a, b, (((1,), (0,)), ((), ())), preferred_element_type=F32)


def nt(a, b):
    return lax.dot_general(a, b, (((1,), (1,)), ((), ())), preferred_element_type=F32)


def tn(a, b):
    return lax.dot_general(a, b, (((0,), (0,)), ((), ())), preferred_element_type=F32)


def rows_mean(v):
    return jnp.mean(v, axis=-1, keepdims=True)


def norm_stats(v):
    mean = rows_mean(v)
    centered = v - mean
    inv_std = lax.rsqrt(rows_mean(centered * centered) + EPS)
    return mean, inv_std, centered * inv_std


def norm_back(dy, hat, inv_std, gain):
    scaled = dy * gain
    return inv_std * (scaled - rows_mean(scaled) - hat * rows_mean(scaled * hat))


def fold8(v):
    return jnp.sum(v.reshape(v.shape[0] // 8, 8, v.shape[1]), axis=0)


class Plan:
    def __init__(self, mesh, media, latents, up):
        self.N = mesh.shape["narrow"]
        self.W = mesh.shape["wide"]
        self.X = self.N // 2
        self.W2 = self.W // 2
        self.Mo, self.D = media.shape[1], media.shape[2]
        self.Lo = latents.shape[1]
        self.M = self.Mo * self.N
        self.L = self.Lo * self.N
        self.HL = HEADS // self.N
        self.C = self.HL * HEAD_DIM
        self.KT = self.M + -(-self.L // LANES) * LANES
        self.F = up.shape[1]
        self.S = self.D // self.W
        self.V = self.S // self.N
        self.R = self.HL * self.L
        self.CH = 128
        self.NC = self.Mo // self.CH
        self.reuse = self.F == self.D and self.X * self.Mo <= self.D


def body_kernel(p, sem_counts, *refs):
    (
        media_h, lat_ref, fc_ref, mm_ref, te_ref, mg_ref, mb_ref, lg_ref, lb_ref, fg_ref, fb_ref,
        wq_h, wkv_h, wo_ref, up_h, down_h, cot_ref,
        out_lat, out_gm, out_gl, out_vec, out_q, out_kv, out_o, out_up, out_down,
        media, x_all, kvw, wq, wot, up, down, kv, st, pt, pn, gpair, mt, te32, mean_s, istd_s,
        lat_nf, lat_ag, cot_ag, cnt_ag,
        rs_st, rs_rc, hid_ag, gb_ag, mate_st, mate_rc, x_st, x_rc, own_sum,
        kvg, kvg_y, kvg_z, act_g, pre_g, att_g, gq_g, sl_st, sl_rc, ga, acc8, stat, vec_st, vec_rc, vec2_st, vec2_rc,
        o_up, o_down, o_o, o_q, o_kv, o_vec, ssem, rsem, lsem,
    ) = refs
    N, W, X, W2 = p.N, p.W, p.X, p.W2
    Mo, Lo, M, L, D, C, R, S, F, KT = p.Mo, p.Lo, p.M, p.L, p.D, p.C, p.R, p.S, p.F, p.KT
    CH, NC, HL, V = p.CH, p.NC, p.HL, p.V
    n = lax.axis_index("narrow")
    w = lax.axis_index("wide")
    core = lax.rem(n, 2)
    xpos = lax.div(n, 2)
    mate = n + 1 - 2 * core
    par = lax.rem(w, 2)
    partner = w + 1 - 2 * par
    scale = HEAD_DIM ** (-0.5)

    if p.reuse:
        mate_st, x_st = up, down

    counters = {"s": 0, "r": 0, "l": 0}
    sends = []
    local = []

    def new(kind, count=1):
        base = counters[kind]
        counters[kind] = base + count
        return base

    def put(src, dst, recv, axis, peer):
        d = pltpu.make_async_remote_copy(
            src, dst, ssem.at[new("s")], rsem.at[recv], device_id={axis: peer}, device_id_type=MESH
        )
        d.start()
        sends.append(d)

    def got(dst, recv):
        pltpu.make_async_remote_copy(
            dst, dst, ssem.at[0], rsem.at[recv], device_id={"narrow": mate}, device_id_type=MESH
        ).wait_recv()

    def here(src, dst, keep=True):
        d = pltpu.make_async_copy(src, dst, lsem.at[new("l")])
        d.start()
        if keep:
            local.append(d)
        return d

    def rows(ref, start, count):
        return ref.at[pl.ds(start, count), :]

    def al(v, m):
        return pl.multiple_of(v, m)

    def npeer(k):
        return lax.rem(n + k, N)

    def nsrc(k):
        return lax.rem(n + N - k, N)

    def wpeer(k):
        return lax.rem(w + k, W)

    def wsrc(k):
        return lax.rem(w + W - k, W)

    media_in = [here(rows(media_h, c * CH, CH), rows(media, c * CH, CH), False) for c in range(NC)]
    down_in = here(down_h, down, False)
    up_in = here(up_h, up, False)

    barrier = pltpu.get_barrier_semaphore()
    for k in range(1, N):
        pl.semaphore_signal(barrier, inc=1, device_id={"narrow": npeer(k)}, device_id_type=MESH)
    for k in range(1, W):
        pl.semaphore_signal(barrier, inc=1, device_id={"wide": wpeer(k)}, device_id_type=MESH)
    pl.semaphore_wait(barrier, N - 1 + W - 1)

    def wide_gather(src, buf, count):
        at = lambda b: rows(buf, al(b * count, 16), count)
        direct = new("r", W2)
        fwd = new("r", W2)
        for k in range(1, W2):
            put(src, at(w), direct + k, "wide", wpeer(2 * k))
        put(src, at(w), direct, "wide", partner)

        def forward(k):
            b = wsrc(2 * k)
            got(at(b), direct + k)
            put(at(b), at(b), fwd + k, "wide", partner)

        def finish():
            got(at(partner), direct)
            for k in range(1, W2):
                b = lax.rem(partner + W - 2 * k, W)
                got(at(b), fwd + k)

        return forward, finish

    own_w = [
        here(wkv_h, rows(kvw, al(w * S, 16), S), False),
        here(wq_h, rows(wq, al(w * S, 16), S), False),
    ]
    kv_fwd, kv_fin = wide_gather(wkv_h, kvw, S)
    q_fwd, q_fin = wide_gather(wq_h, wq, S)

    lat = lat_ref[...].astype(F32)
    lat_mean, lat_istd, lat_hat = norm_stats(lat)
    lat_ag[n] = (lat_hat * lg_ref[...] + lb_ref[...]).astype(BF16)
    cot_ag[n] = cot_ref[...]

    def narrow_gather(buf):
        base = new("r", N)
        for k in range(1, N):
            put(buf.at[n], buf.at[n], base + k, "narrow", npeer(k))

        def finish():
            for k in range(1, N):
                got(buf.at[nsrc(k)], base + k)
            return jnp.concatenate([buf[i].astype(F32) for i in range(N)], axis=0).astype(BF16)

        return finish

    te32[...] = te_ref[...].astype(F32)
    gain_m, bias_m = mg_ref[...], mb_ref[...]

    m_direct = new("r", NC * X)
    m_fwd = new("r", NC * X)

    def m_rows(block, c):
        return rows(x_all, al(block * Mo + c * CH, 16), CH)

    def frame_of(c):
        return lax.div(n * Mo + c * CH, PATCHES)

    for c in range(NC):
        media_in[c].wait()
        te_row = te32[pl.ds(frame_of(c), 1), :]

        def norm_rows(i, carry, c=c, te_row=te_row):
            r = al(c * CH + i * 16, 16)
            v = media[pl.ds(r, 16), :].astype(F32) + te_row
            mean, inv_std, hat = norm_stats(v)
            mean_s[pl.ds(r, 16), :] = jnp.broadcast_to(mean, (16, LANES))
            istd_s[pl.ds(r, 16), :] = jnp.broadcast_to(inv_std, (16, LANES))
            x_all[pl.ds(al(n * Mo + r, 16), 16), :] = (hat * gain_m + bias_m).astype(BF16)
            return carry

        lax.fori_loop(0, CH // 16, norm_rows, 0, unroll=2)
        for j in range(1, X):
            peer = lax.rem(xpos + j, X) * 2 + core
            put(m_rows(n, c), m_rows(n, c), m_direct + c * X + j, "narrow", peer)
        put(m_rows(n, c), m_rows(n, c), m_direct + c * X, "narrow", mate)
        if c == 0:
            lat_fin = narrow_gather(lat_ag)
            cot_fin = narrow_gather(cot_ag)

    def media_forward(c):
        for j in range(1, X):
            block = lax.rem(xpos + X - j, X) * 2 + core
            got(m_rows(block, c), m_direct + c * X + j)
            put(m_rows(block, c), m_rows(block, c), m_fwd + c * X + j, "narrow", mate)

    wot_st = wo_ref[...].astype(F32).T.astype(BF16)
    wot[pl.ds(al(w * S, 16), S), :] = wot_st

    slot_frame = lax.div(lax.broadcasted_iota(jnp.int32, (M // LANES, LANES), 0), PATCHES // LANES)
    ok = (slot_frame < fc_ref[0]) & (mm_ref[...] > 0)
    okf = jnp.where(ok, 1.0, 0.0).astype(F32)
    tail = jnp.where(
        lax.broadcasted_iota(jnp.int32, (1, KT - M), 1) < L, 1.0, 0.0
    ).astype(F32)
    for j in range(KT // LANES):
        row = okf[j : j + 1, :] if j < M // LANES else tail[:, j * LANES - M : j * LANES - M + LANES]
        mt[j * LANES : (j + 1) * LANES, :] = jnp.broadcast_to(row, (LANES, LANES)).T
    count = jnp.sum(okf, keepdims=True) + float(L)
    cnt_ag[w] = jnp.broadcast_to(count, (8, LANES))
    cnt_base = new("r", W)
    for k in range(1, W):
        put(cnt_ag.at[w], cnt_ag.at[w], cnt_base + k, "wide", wpeer(k))

    kv_fwd(1)
    o_fwd, o_fin = wide_gather(rows(wot, al(w * S, 16), S), wot, S)
    for k in range(2, W2):
        kv_fwd(k)
    media_forward(0)

    def spread(which, value):
        for b in range(W):
            sl_st[which, b * L : (b + 1) * L, :] = value[:, b * S : (b + 1) * S]
        base = new("r", W)
        at = lambda ref, b: ref.at[which, pl.ds(al(b * L, 16), L), :]
        for k in range(1, W):
            put(at(sl_st, wpeer(k)), at(sl_rc, w), base + k, "wide", wpeer(k))
        sl_rc[which, pl.ds(al(w * L, 16), L), :] = sl_st[which, pl.ds(al(w * L, 16), L), :]

        def finish():
            for k in range(1, W):
                got(at(sl_rc, wsrc(k)), base + k)

        return finish

    lat_all = lat_fin()
    cot_all = cot_fin()
    x_all[M : M + L, :] = lat_all
    if KT > M + L:
        x_all[M + L : KT, :] = jnp.zeros((KT - M - L, D), BF16)
    slat_fin = spread(0, lat_all)
    scot_fin = spread(1, cot_all)

    down_in.wait()

    def act_grad(j, carry):
        r = al(j * 256, 256)
        ga[:, pl.ds(r, 256)] = nt(cot_all, down[pl.ds(r, 256), :])
        return carry

    lax.fori_loop(0, F // 256, act_grad, 0)

    for k in range(1, W2):
        q_fwd(k)
    if NC > 1:
        media_forward(1)
    for d in own_w:
        d.wait()
    kv_fin()

    def project(start, count):
        def step(i, carry):
            r = al(start + i * CH, 16)
            kv[pl.ds(r, CH), :] = nn(x_all[pl.ds(r, CH), :], kvw[...]).astype(BF16)
            return carry

        lax.fori_loop(0, count // CH, step, 0)

    project(n * Mo, Mo)
    project(M, KT - M)
    for k in range(1, W2):
        o_fwd(k)
    for c in range(NC):
        got(m_rows(mate, c), m_direct + c * X)
    project(mate * Mo, Mo)
    q_fin()
    q_act = nn(lat_all, wq[...]).astype(BF16).astype(F32)
    head_of = lax.div(lax.broadcasted_iota(jnp.int32, (L, C), 1), HEAD_DIM)

    def per_head(v):
        return jnp.concatenate([jnp.where(head_of == h, v, 0.0) for h in range(HL)], axis=0)

    def from_heads(v):
        total = jnp.where(head_of == 0, v[0:L], 0.0)
        for h in range(1, HL):
            total = total + jnp.where(head_of == h, v[h * L : (h + 1) * L], 0.0)
        return total

    q_big32 = per_head(q_act)
    q_big = q_big32.astype(BF16)
    q_big_t = q_big32.T.astype(BF16)
    for c in range(2, NC):
        media_forward(c)
    for c in range(NC):
        for j in range(1, X):
            block = lax.rem(xpos + X - j, X) * 2 + core
            project(block * Mo + c * CH, CH)
            block = lax.rem(xpos + X - j, X) * 2 + 1 - core
            got(m_rows(block, c), m_fwd + c * X + j)
            project(block * Mo + c * CH, CH)

    KB = 128

    def wide_mask(r):
        m = mt[pl.ds(r, KB), :]
        return jnp.concatenate([m] * (R // LANES), axis=1) > 0.0

    def score_step(j, top):
        r = al(j * KB, KB)
        s = nn(kv[pl.ds(r, KB), 0:C], q_big_t) * scale
        s = jnp.where(wide_mask(r), s, NEG)
        st[pl.ds(r, KB), :] = s
        return jnp.maximum(top, jnp.max(s, axis=0, keepdims=True))

    top = lax.fori_loop(0, KT // KB, score_step, jnp.full((1, R), NEG, F32))

    def exp_step(j, carry):
        total, dot = carry
        r = al(j * KB, KB)
        s = st[pl.ds(r, KB), :]
        e = jnp.exp(s - top)
        pt[pl.ds(r, KB), :] = e
        s = jnp.where(wide_mask(r), s, 0.0)
        st[pl.ds(r, KB), :] = s
        return (
            total + jnp.sum(e, axis=0, keepdims=True),
            dot + jnp.sum(e * s, axis=0, keepdims=True),
        )

    zero_row = jnp.zeros((1, R), F32)
    total, dot = lax.fori_loop(0, KT // KB, exp_step, (zero_row, zero_row))
    inv_total = 1.0 / total
    mean_score = dot * inv_total

    def prob_step(j, carry):
        r = al(j * KB, KB)
        pr = pt[pl.ds(r, KB), :] * inv_total
        pt[pl.ds(r, KB), :] = pr
        pn[:, pl.ds(r, KB)] = pr.T.astype(BF16)
        return carry

    lax.fori_loop(0, KT // KB, prob_step, 0)
    attn = from_heads(nn(pn[...], kv[:, C : 2 * C]))
    attn_low = attn.astype(BF16)

    at_w = lambda ref: rows(ref, al(w * L, 16), L)
    att_g[pl.ds(al(w * L, 16), L), :] = attn_low

    def narrow_sum(slot, parts):
        base = new("r", N)
        for k in range(1, N):
            put(rs_st.at[slot, npeer(k)], rs_rc.at[slot, k], base + k, "narrow", npeer(k))

        def finish():
            v = rs_st[slot, n].astype(F32)
            for k in range(1, N):
                got(rs_rc.at[slot, k], base + k)
                v = v + rs_rc[slot, k].astype(F32)
            return v

        return finish

    def stage(slot, cols, v):
        for i in range(N):
            rs_st[slot, i, :, cols] = v[i * Lo : (i + 1) * Lo].astype(BF16)

    for d in (o_fin,):
        d()

    def branch_step(j, carry):
        r = al(j * 256, 256)
        stage(0, pl.ds(r, 256), nt(attn_low, wot[pl.ds(r, 256), :]))
        return carry

    lax.fori_loop(0, D // 256, branch_step, 0)
    branch_fin = narrow_sum(0, None)
    att_fwd, att_fin = wide_gather(at_w(att_g), att_g, L)
    mid = lat + branch_fin()
    mid_mean, mid_istd, mid_hat = norm_stats(mid)
    hid_ag[n] = (mid_hat * fg_ref[...] + fb_ref[...]).astype(BF16)
    hid_fin = narrow_gather(hid_ag)
    up_in.wait()
    hid_all = hid_fin()

    own64 = pl.ds(al(w * L, 16), L)

    def ffn_step(j, carry):
        cs = pl.ds(al(j * 256, 256), 256)
        pre = nn(hid_all, up[:, cs])
        cdf = 0.5 * (1.0 + lax.erf(pre * (1.0 / math.sqrt(2.0))))
        density = jnp.exp(-0.5 * pre * pre) * (1.0 / math.sqrt(2.0 * math.pi))
        act_g[own64, cs] = (pre * cdf).astype(BF16)
        pre_g[own64, cs] = (ga[:, cs] * (cdf + pre * density)).astype(BF16)
        return carry

    lax.fori_loop(0, F // 256, ffn_step, 0)
    gpre = pre_g[own64, :]

    def hid_back(j, carry):
        r = al(j * 256, 256)
        stage(1, pl.ds(r, 256), nt(gpre, up[pl.ds(r, 256), :]))
        return carry

    lax.fori_loop(0, D // 256, hid_back, 0)
    ghid_fin = narrow_sum(1, None)
    act_fwd, act_fin = wide_gather(at_w(act_g), act_g, L)
    pre_fwd, pre_fin = wide_gather(at_w(pre_g), pre_g, L)
    act_own = act_g[own64, :]

    def ffn_out(j, carry):
        cs = pl.ds(al(j * 256, 256), 256)
        stage(2, cs, nn(act_own, down[:, cs]))
        return carry

    lax.fori_loop(0, D // 256, ffn_out, 0)
    ffn_fin = narrow_sum(2, None)
    shid_fin = spread(2, hid_all)

    ghid = ghid_fin()
    grad_mid = cot_ref[...].astype(F32) + norm_back(ghid, mid_hat, mid_istd, fg_ref[...])
    gb_ag[n] = grad_mid.astype(BF16)
    gb_fin = narrow_gather(gb_ag)
    acc8[...] = jnp.zeros_like(acc8)
    stat[...] = jnp.zeros_like(stat)
    stat[FRAMES_MAX + 4 : FRAMES_MAX + 5, :] = jnp.sum(ghid * mid_hat, axis=0, keepdims=True)
    stat[FRAMES_MAX + 5 : FRAMES_MAX + 6, :] = jnp.sum(ghid, axis=0, keepdims=True)
    for k in range(1, W2):
        att_fwd(k)
    for k in range(1, W):
        got(cnt_ag.at[wsrc(k)], cnt_base + k)
    keys = cnt_ag[0]
    for i in range(1, W):
        keys = keys + cnt_ag[i]
    ent1 = ENT_COEF * float(W * M) / keys[0:1, :]
    ent = jnp.concatenate([ent1] * (R // LANES), axis=1)
    gb_all = gb_fin()

    g_attn = nn(gb_all, wot[...]).astype(BF16).astype(F32)
    g_big32 = per_head(g_attn)
    g_big = g_big32.astype(BF16)
    g_big_t = g_big32.T.astype(BF16)
    row_dot = jnp.sum(per_head(g_attn * attn).T, axis=0, keepdims=True)
    shift = row_dot - ent * mean_score

    def back_step(j, carry):
        r = al(j * KB, KB)
        pr = pt[pl.ds(r, KB), :]
        gp = nn(kv[pl.ds(r, KB), C : 2 * C], g_big_t)
        gs = pr * (gp - ent * st[pl.ds(r, KB), :] - shift)
        pn[:, pl.ds(r, KB)] = gs.T.astype(BF16)
        gpair[pl.ds(r, KB), 0:C] = (nn(gs.astype(BF16), q_big) * scale).astype(BF16)
        gpair[pl.ds(r, KB), C : 2 * C] = nn(pr.astype(BF16), g_big).astype(BF16)
        return carry

    lax.fori_loop(0, KT // KB, back_step, 0)

    mate_base = new("r", X * NC)
    xs_base = new("r", X * NC)

    def part(block, c):
        r = al(block * Mo + c * CH, 16)
        return nt(gpair[pl.ds(r, CH), :], kvw[...])

    def x_of(j):
        return lax.rem(xpos + j, X)

    def to_mate(j, c):
        b = x_of(j) * 2 + 1 - core
        mate_st[(j * NC + c) * CH : (j * NC + c + 1) * CH, :] = part(b, c).astype(BF16)
        piece = lambda ref: rows(ref, (j * NC + c) * CH, CH)
        put(piece(mate_st), piece(mate_rc), mate_base + j * NC + c, "narrow", mate)

    def from_mate(j, c):
        i = (j * NC + c) * CH
        got(rows(mate_rc, i, CH), mate_base + j * NC + c)
        return part(x_of(j) * 2 + core, c) + mate_rc[i : i + CH, :].astype(F32)

    for j in range(1, X):
        for c in range(NC):
            to_mate(j, c)
        for c in range(NC):
            i = ((j - 1) * NC + c) * CH
            x_st[i : i + CH, :] = from_mate(j, c).astype(BF16)
            put(
                rows(x_st, i, CH), rows(x_rc, i, CH), xs_base + (j - 1) * NC + c,
                "narrow", x_of(j) * 2 + core,
            )
    for k in range(1, W2):
        act_fwd(k)
        pre_fwd(k)

    gq = (from_heads(nn(pn[...], kv[:, 0:C])) * scale).astype(BF16)
    gq_g[own64, :] = gq
    gpl = gpair[M : M + L, :]

    def lat_back(j, carry):
        r = al(j * 256, 256)
        stage(3, pl.ds(r, 256), nt(gpl, kvw[pl.ds(r, 256), :]) + nt(gq, wq[pl.ds(r, 256), :]))
        return carry

    lax.fori_loop(0, D // 256, lat_back, 0)
    glat_fin = narrow_sum(3, None)
    gq_fwd, gq_fin = wide_gather(at_w(gq_g), gq_g, L)
    sgb_fin = spread(3, gb_all)

    def kvg_step(j, carry):
        r = al(j * 256, 256)
        kvg[pl.ds(r, 256), :] = tn(x_all[:, pl.ds(r, 256)], gpair[...]).astype(BF16)
        return carry

    lax.fori_loop(0, D // 256, kvg_step, 0)
    y_base = new("r", W2)
    z_base = new("r", W2)
    kb = lambda g, q: rows(kvg, al((2 * g + q) * S, 16), S)
    for g in range(W2):
        put(kb(g, 1 - par), rows(kvg_y, g * S, S), y_base + g, "wide", partner)

    for c in range(NC):
        to_mate(0, c)
    for c in range(NC):
        own_sum[c * CH : (c + 1) * CH, :] = from_mate(0, c)

    half = lax.div(w, 2)
    for k in list(range(1, W2)) + [0]:
        g = lax.rem(half + k, W2)
        yr = rows(kvg_y, al(g * S, 16), S)
        got(yr, y_base) if W2 == 1 else None
        if W2 > 1:
            pltpu.make_async_remote_copy(
                yr, yr, ssem.at[0], rsem.at[y_base + g], device_id={"narrow": mate}, device_id_type=MESH
            ).wait_recv()
        mine = pl.ds(al((2 * g + par) * S, 16), S)
        summed = kvg[mine, :].astype(F32) + kvg_y[pl.ds(al(g * S, 16), S), :].astype(F32)
        if k:
            kvg[mine, :] = summed.astype(BF16)
            put(rows(kvg, al((2 * g + par) * S, 16), S), rows(kvg_z, k * S, S), z_base + k, "wide", 2 * g + par)
        else:
            o_kv[...] = summed

    out_l = (mid + ffn_fin()).astype(BF16)
    lat_nf[0] = out_l
    here(lat_nf.at[0], out_lat)
    glat = glat_fin()
    g_lat = grad_mid + norm_back(glat, lat_hat, lat_istd, lg_ref[...])
    lat_nf[1] = g_lat.astype(BF16)
    here(lat_nf.at[1], out_gl)
    stat[FRAMES_MAX + 2 : FRAMES_MAX + 3, :] = jnp.sum(glat * lat_hat, axis=0, keepdims=True)
    stat[FRAMES_MAX + 3 : FRAMES_MAX + 4, :] = jnp.sum(glat, axis=0, keepdims=True)

    for k in range(1, W2):
        gq_fwd(k)
    att_fin()
    sgb_fin()
    o_o[...] = tn(att_g[...], sl_rc[3])
    here(o_o, out_o)
    act_fin()
    scot_fin()

    def down_step(j, carry):
        r = al(j * 256, 256)
        o_down[pl.ds(r, 256), :] = tn(act_g[:, pl.ds(r, 256)], sl_rc[1])
        return carry

    lax.fori_loop(0, F // 256, down_step, 0)
    here(o_down, out_down)
    pre_fin()
    shid_fin()

    def up_step(j, carry):
        cs = pl.ds(al(j * 256, 256), 256)
        o_up[:, cs] = tn(sl_rc[2], pre_g[:, cs])
        return carry

    lax.fori_loop(0, F // 256, up_step, 0)
    here(o_up, out_up)
    gq_fin()
    slat_fin()
    o_q[...] = tn(sl_rc[0], gq_g[...])
    here(o_q, out_q)

    gm_out = []
    for c in range(NC):
        for j in range(1, X):
            i = ((j - 1) * NC + c) * CH
            got(rows(x_rc, i, CH), xs_base + (j - 1) * NC + c)
        f = frame_of(c)
        te_row = te32[pl.ds(f, 1), :]

        def back_rows(i, carry, c=c, te_row=te_row):
            r = al(c * CH + i * 16, 16)
            dy = own_sum[pl.ds(r, 16), :]
            for j in range(1, X):
                dy = dy + x_rc[pl.ds(al((j - 1) * Mo + r, 16), 16), :].astype(F32)
            mean = mean_s[pl.ds(r, 16), 0:1]
            inv_std = istd_s[pl.ds(r, 16), 0:1]
            hat = (media[pl.ds(r, 16), :].astype(F32) + te_row - mean) * inv_std
            dx = norm_back(dy, hat, inv_std, gain_m)
            media[pl.ds(r, 16), :] = dx.astype(BF16)
            acc8[0:8, :] += fold8(dy * hat)
            acc8[8:16, :] += fold8(dy)
            acc8[16:24, :] += fold8(dx)
            return carry

        lax.fori_loop(0, CH // 16, back_rows, 0)
        stat[pl.ds(f, 1), :] += jnp.sum(acc8[16:24, :], axis=0, keepdims=True)
        acc8[16:24, :] = jnp.zeros((8, D), F32)
        here(rows(media, c * CH, CH), rows(out_gm, c * CH, CH))
    stat[FRAMES_MAX : FRAMES_MAX + 1, :] = jnp.sum(acc8[0:8, :], axis=0, keepdims=True)
    stat[FRAMES_MAX + 1 : FRAMES_MAX + 2, :] = jnp.sum(acc8[8:16, :], axis=0, keepdims=True)

    vec = stat[...]
    for b in range(W):
        vec_st[b] = vec[:, b * S : (b + 1) * S]
    v_base = new("r", W)
    for k in range(1, W):
        put(vec_st.at[wpeer(k)], vec_rc.at[k], v_base + k, "wide", wpeer(k))
    for k in range(1, W2):
        got(rows(kvg_z, k * S, S), z_base + k)
        o_kv[...] += kvg_z[k * S : (k + 1) * S, :].astype(F32)
    here(o_kv, out_kv)
    vs = vec_st[w]
    for k in range(1, W):
        got(vec_rc.at[k], v_base + k)
        vs = vs + vec_rc[k]
    for i in range(N):
        vec2_st[i] = vs[:, i * V : (i + 1) * V]
    v2_base = new("r", N)
    for k in range(1, N):
        put(vec2_st.at[npeer(k)], vec2_rc.at[k], v2_base + k, "narrow", npeer(k))
    vs = vec2_st[n]
    for k in range(1, N):
        got(vec2_rc.at[k], v2_base + k)
        vs = vs + vec2_rc[k]
    o_vec[...] = vs
    here(o_vec, out_vec)

    for d in sends:
        d.wait_send()
    for d in local:
        d.wait()
    sem_counts.update(counters)


def make_body(mesh):
    def body(
        media_feats, latents, frame_counts, media_mask, time_embed, media_gain, media_bias, latent_gain,
        latent_bias, ffn_gain, ffn_bias, query_weight, keyval_weight, output_weight, up_weight,
        down_weight, cotangent,
    ):
        p = Plan(mesh, media_feats, latents, up_weight)
        D, C, S, L, Lo, KT, R, F, N, W, Mo = p.D, p.C, p.S, p.L, p.Lo, p.KT, p.R, p.F, p.N, p.W, p.Mo
        X, W2, NC, V = p.X, p.W2, p.NC, p.V
        vm = pl.BlockSpec(memory_space=pltpu.VMEM)
        hbm = pl.BlockSpec(memory_space=pl.ANY)
        smem = pl.BlockSpec(memory_space=pltpu.SMEM)
        row = lambda v: v.reshape(1, D)
        sds = jax.ShapeDtypeStruct
        vmem = pltpu.VMEM
        scratch = [
            vmem((Mo, D), BF16),
            vmem((KT, D), BF16),
            vmem((D, 2 * C), BF16),
            vmem((D, C), BF16),
            vmem((D, C), BF16),
            vmem((D, F), BF16),
            vmem((F, D), BF16),
            vmem((KT, 2 * C), BF16),
            vmem((KT, R), F32),
            vmem((KT, R), F32),
            vmem((R, KT), BF16),
            vmem((KT, 2 * C), BF16),
            vmem((KT, LANES), F32),
            vmem((FRAMES_MAX, D), F32),
            vmem((Mo, LANES), F32),
            vmem((Mo, LANES), F32),
            vmem((2, Lo, D), BF16),
            vmem((N, Lo, D), BF16),
            vmem((N, Lo, D), BF16),
            vmem((W, 8, LANES), F32),
            vmem((4, N, Lo, D), BF16),
            vmem((4, N, Lo, D), BF16),
            vmem((N, Lo, D), BF16),
            vmem((N, Lo, D), BF16),
            vmem((8, LANES) if p.reuse else (X * Mo, D), BF16),
            vmem((X * Mo, D), BF16),
            vmem((8, LANES) if p.reuse else ((X - 1) * Mo, D), BF16),
            vmem(((X - 1) * Mo, D), BF16),
            vmem((Mo, D), F32),
            vmem((D, 2 * C), BF16),
            vmem((W2 * S, 2 * C), BF16),
            vmem((W2 * S, 2 * C), BF16),
            vmem((W * L, F), BF16),
            vmem((W * L, F), BF16),
            vmem((W * L, C), BF16),
            vmem((W * L, C), BF16),
            vmem((4, W * L, S), BF16),
            vmem((4, W * L, S), BF16),
            vmem((L, F), F32),
            vmem((24, D), F32),
            vmem((16, D), F32),
            vmem((W, 16, S), F32),
            vmem((W, 16, S), F32),
            vmem((N, 16, V), F32),
            vmem((N, 16, V), F32),
            vmem((S, F), F32),
            vmem((F, S), F32),
            vmem((C, S), F32),
            vmem((S, C), F32),
            vmem((S, 2 * C), F32),
            vmem((16, V), F32),
            pltpu.SemaphoreType.DMA((24 * W + 8 * N * p.NC + 64,)),
            pltpu.SemaphoreType.DMA((24 * W + 8 * N * p.NC + 64,)),
            pltpu.SemaphoreType.DMA((64,)),
        ]
        outs = pl.pallas_call(
            functools.partial(body_kernel, p, {}),
            out_shape=(
                sds((Lo, D), BF16),
                sds((Mo, D), BF16),
                sds((Lo, D), BF16),
                sds((16, V), F32),
                sds((S, C), F32),
                sds((S, 2 * C), F32),
                sds((C, S), F32),
                sds((S, F), F32),
                sds((F, S), F32),
            ),
            in_specs=[hbm, vm, smem, vm, vm, vm, vm, vm, vm, vm, vm, hbm, hbm, vm, hbm, hbm, vm],
            out_specs=[hbm] * 9,
            scratch_shapes=scratch,
            compiler_params=pltpu.CompilerParams(
                collective_id=0, has_side_effects=True, vmem_limit_bytes=67_043_328
            ),
        )(
            media_feats[0], latents[0], frame_counts, media_mask.reshape(p.M // LANES, LANES), time_embed,
            row(media_gain), row(media_bias), row(latent_gain), row(latent_bias), row(ffn_gain), row(ffn_bias),
            query_weight, keyval_weight.reshape(S, 2 * C), output_weight, up_weight, down_weight, cotangent[0],
        )
        lat, gm, gl, vec, gq, gkv, go, gup, gdown = outs
        return (
            lat[None], gm[None], gl[None], vec[:FRAMES_MAX], vec[FRAMES_MAX], vec[FRAMES_MAX + 1],
            vec[FRAMES_MAX + 2], vec[FRAMES_MAX + 3], vec[FRAMES_MAX + 4], vec[FRAMES_MAX + 5], gq,
            gkv.reshape(S, 2, C), go, gup, gdown,
        )

    return body


def solution(mesh):
    both = P(("wide", "narrow"))
    rows = P("wide", "narrow", None)
    return jax.shard_map(
        make_body(mesh),
        mesh=mesh,
        in_specs=(
            rows, rows, P("wide"), P("wide", None), P(), P(), P(), P(), P(), P(), P(), P("wide", "narrow"),
            P("wide", None, "narrow"), P("narrow", "wide"), P(None, "narrow"), P("narrow", None), rows,
        ),
        out_specs=(
            rows, rows, rows, P(None, ("wide", "narrow")), both, both, both, both, both, both,
            P("wide", "narrow"), P("wide", None, "narrow"), P("narrow", "wide"), P("wide", "narrow"),
            P("narrow", "wide"),
        ),
        check_vma=False,
    )
```

time: 679 us -> 235 us (0.35)
  waiting for transfers between devices: 449 us -> 0 us
  Pallas kernels: 0 us -> 210 us
  matrix products: 79.9 us -> 0 us
  blocking collectives: 44.8 us -> 0 us
  local copies, waits for them, and re-layouts: 58.9 us -> 23 us
  other arithmetic: 21.2 us -> 0 us
  between operations: 16.9 us -> 1.33 us
    all_gather x5 -> x0, waiting for transfers between devices: 210 us -> none  [the longest x1 69.3 us: body(): lax.all_gather(jnp.concatenate([act_low, grad_pre, attn_low, grad_query],...]
    pallas_call x0 -> x1, Pallas kernels: none -> 210 us  [body(): pl.pallas_call(functools.partial(body_kernel, p, {}), out_shape=(sds((Lo,...]
    reduce_scatter x6 -> x0, waiting for transfers between devices: 108 us -> none  [the longest x1 52.1 us: body(): lax.psum_scatter(rows_part[:media_total].astype(bf16), 'narrow', scatter_...]
    unnamed x13 -> x0, waiting for transfers between devices: 96.5 us -> none
    dot_general x23 -> x0, matrix products: 76.3 us -> none  [the longest x21 73 us: mm(): return jnp.einsum(spec, a, b, preferred_element_type=f32)]
    all_to_all x1 -> x0, waiting for transfers between devices: 33.9 us -> none  [body(): cut = lax.all_to_all(cut, 'wide', split_axis=0, concat_axis=0, tiled=True)]
    all_gather x4 -> x0, blocking collectives: 25.2 us -> none  [the longest x1 7.1 us: body(): cot_all = lax.all_gather(cot_one, 'narrow', axis=0, tiled=True)]
    psum x1 -> x0, blocking collectives: 19.6 us -> none  [body(): total_count = lax.psum(local_count, 'wide')]
  transfers between devices with their start and end apart: 13 -> 0, of which waited for: 11 -> 0; matrix products, arithmetic and copies ran while one was open for 14% -> 0% of each run, Pallas kernels for 0% -> 0%
where the time goes in v2:
time: 235 us; the launch traced here: 234 us
  Pallas kernels  210 us (89%)
  local copies, waits for them, and re-layouts  23 us (10%)
    pallas_call x1, Pallas kernels, body(): pl.pallas_call(functools.partial(body_kernel, p, {}), out_shape=(sds((Lo,...  210 us
    unnamed x23, local copies, waits for them, and re-layouts  11.4 us
    reshape x6, local copies, waits for them, and re-layouts, body(): row = lambda v: v.reshape(1, D)  7.76 us

profile of v2, /device:TPU:0, one launch (start us, length us, event | category | flops | bytes accessed | tf_op | source)
XLA Modules:
  0.0 234.0 jit_solution(9011944747737596606)
XLA Ops:
  0.6 1.7 copy.35
  2.4 1.7 copy.32.refs_13_
  4.1 1.3 reshape.58.refs_5_
  5.4 1.3 reshape.59.refs_6_
  6.7 1.3 reshape.60.refs_7_
  8.0 1.3 reshape.61.refs_8_
  9.3 1.3 reshape.62.refs_9_
  10.5 1.3 reshape.63.refs_10_
  12.5 209.7 %shard_map.280 = (bf16[16,1536]{1,0:T(8,128)(2,1)}, bf16[512,1536]{1,0:T(8,128)(2,1)}, bf16[16,1536]{1,0:T(8,128)(2,1)}, f32[16,48]{1,0:T(8,128)}, f32[192,384]{...) custom-call(bf16[512,1536]{1,0:T(8,128)(2,1)} %bitcast.22, ...), custom_call_target="tpu_custom_call" | custom-call | tf_op jit(solution)/shard_map/pallas_call | solution.py:764
  222.2 0.0 copy-start.2
  222.2 1.4 slice_bitcast_fusion
  223.6 1.3 slice.21
  224.9 0.0 copy-start.3
  224.9 2.9 %copy.34 = f32[1536,192]{0,1:T(8,128)} copy(f32[1536,192]{1,0:T(8,128)} %get-tuple-element.47) | data formatting | bytes 2359296
  227.8 0.0 copy-start.6
  227.8 0.0 copy-start
  227.8 0.0 copy-done.2
  227.8 1.1 reshape.65
  229.0 0.0 copy-done.3
  229.0 0.9 copy.33
  229.8 0.0 copy-done.6
  229.8 0.6 copy.42
  230.5 0.0 copy-done
  230.5 0.0 copy-start.5
  230.5 0.0 copy-start.4
  230.5 0.0 copy-start.1
  230.5 1.1 copy.43
  231.6 0.0 copy-done.5
  231.6 0.6 copy.44
  232.2 0.0 copy-done.4
  232.2 0.7 copy.45
  232.9 0.0 copy-done.1
  233.0 1.0 copy.46
Async XLA Ops:
  222.2 5.7 %copy-start.2 = (f32[192,768]{1,0:T(8,128)S(1)}, f32[192,768]{1,0:T(8,128)}, u32[]{:S(2)}) copy-start(f32[192,768]{1,0:T(8,128)} %get-tuple-element.29) | copy-start | bytes 1769476
  224.9 4.1 %copy-start.3 = (f32[384,192]{1,0:T(8,128)S(1)}, f32[384,192]{1,0:T(8,128)}, u32[]{:S(2)}) copy-start(f32[384,192]{1,0:T(8,128)} %get-tuple-element.45) | copy-start | bytes 884740
  227.8 2.0 copy-start.6
  227.8 2.6 %copy-start = (bf16[512,1536]{1,0:T(8,128)(2,1)S(1)}, bf16[512,1536]{1,0:T(8,128)(2,1)}, u32[]{:S(2)}) copy-start(bf16[512,1536]{1,0:T(8,128)(2,1)} %get-tuple-element.25) | copy-start | bytes 4718596
  230.5 1.2 copy-start.5
  230.5 1.8 copy-start.4
  230.5 2.5 %copy-start.1 = (f32[192,1536]{1,0:T(8,128)S(1)}, f32[192,1536]{1,0:T(8,128)}, u32[]{:S(2)}) copy-start(f32[192,1536]{1,0:T(8,128)} %get-tuple-element.82) | copy-start | bytes 3538948

commit v3 on v2

--- a/solution.py
+++ b/solution.py
@@ -78,7 +78,7 @@
 def body_kernel(p, sem_counts, *refs):
     (
         media_h, lat_ref, fc_ref, mm_ref, te_ref, mg_ref, mb_ref, lg_ref, lb_ref, fg_ref, fb_ref,
-        wq_h, wkv_h, wo_ref, up_h, down_h, cot_ref,
+        wq_h, wkv_ref, wot_h, up_h, down_h, cot_ref,
         out_lat, out_gm, out_gl, out_vec, out_q, out_kv, out_o, out_up, out_down,
         media, x_all, kvw, wq, wot, up, down, kv, st, pt, pn, gpair, mt, te32, mean_s, istd_s,
         lat_nf, lat_ag, cot_ag, cnt_ag,
@@ -97,6 +97,9 @@
     par = lax.rem(w, 2)
     partner = w + 1 - 2 * par
     scale = HEAD_DIM ** (-0.5)
+    gain_m, bias_m, gain_l, bias_l, gain_f, bias_f = (
+        ref[...].reshape(1, D) for ref in (mg_ref, mb_ref, lg_ref, lb_ref, fg_ref, fb_ref)
+    )
 
     if p.reuse:
         mate_st, x_st = up, down
@@ -150,6 +153,10 @@
     media_in = [here(rows(media_h, c * CH, CH), rows(media, c * CH, CH), False) for c in range(NC)]
     down_in = here(down_h, down, False)
     up_in = here(up_h, up, False)
+
+    wkv = wkv_ref[...].astype(F32)
+    kvw[pl.ds(al(w * S, 16), S), 0:C] = wkv[:, 0, :].astype(BF16)
+    kvw[pl.ds(al(w * S, 16), S), C : 2 * C] = wkv[:, 1, :].astype(BF16)
 
     barrier = pltpu.get_barrier_semaphore()
     for k in range(1, N):
@@ -180,15 +187,16 @@
         return forward, finish
 
     own_w = [
-        here(wkv_h, rows(kvw, al(w * S, 16), S), False),
         here(wq_h, rows(wq, al(w * S, 16), S), False),
+        here(wot_h, rows(wot, al(w * S, 16), S), False),
     ]
-    kv_fwd, kv_fin = wide_gather(wkv_h, kvw, S)
+    kv_fwd, kv_fin = wide_gather(rows(kvw, al(w * S, 16), S), kvw, S)
     q_fwd, q_fin = wide_gather(wq_h, wq, S)
+    o_fwd, o_fin = wide_gather(wot_h, wot, S)
 
     lat = lat_ref[...].astype(F32)
     lat_mean, lat_istd, lat_hat = norm_stats(lat)
-    lat_ag[n] = (lat_hat * lg_ref[...] + lb_ref[...]).astype(BF16)
+    lat_ag[n] = (lat_hat * gain_l + bias_l).astype(BF16)
     cot_ag[n] = cot_ref[...]
 
     def narrow_gather(buf):
@@ -204,7 +212,6 @@
         return finish
 
     te32[...] = te_ref[...].astype(F32)
-    gain_m, bias_m = mg_ref[...], mb_ref[...]
 
     m_direct = new("r", NC * X)
     m_fwd = new("r", NC * X)
@@ -242,9 +249,6 @@
             block = lax.rem(xpos + X - j, X) * 2 + core
             got(m_rows(block, c), m_direct + c * X + j)
             put(m_rows(block, c), m_rows(block, c), m_fwd + c * X + j, "narrow", mate)
-
-    wot_st = wo_ref[...].astype(F32).T.astype(BF16)
-    wot[pl.ds(al(w * S, 16), S), :] = wot_st
 
     slot_frame = lax.div(lax.broadcasted_iota(jnp.int32, (M // LANES, LANES), 0), PATCHES // LANES)
     ok = (slot_frame < fc_ref[0]) & (mm_ref[...] > 0)
@@ -262,7 +266,6 @@
         put(cnt_ag.at[w], cnt_ag.at[w], cnt_base + k, "wide", wpeer(k))
 
     kv_fwd(1)
-    o_fwd, o_fin = wide_gather(rows(wot, al(w * S, 16), S), wot, S)
     for k in range(2, W2):
         kv_fwd(k)
     media_forward(0)
@@ -426,7 +429,7 @@
     att_fwd, att_fin = wide_gather(at_w(att_g), att_g, L)
     mid = lat + branch_fin()
     mid_mean, mid_istd, mid_hat = norm_stats(mid)
-    hid_ag[n] = (mid_hat * fg_ref[...] + fb_ref[...]).astype(BF16)
+    hid_ag[n] = (mid_hat * gain_f + bias_f).astype(BF16)
     hid_fin = narrow_gather(hid_ag)
     up_in.wait()
     hid_all = hid_fin()
@@ -466,7 +469,7 @@
     shid_fin = spread(2, hid_all)
 
     ghid = ghid_fin()
-    grad_mid = cot_ref[...].astype(F32) + norm_back(ghid, mid_hat, mid_istd, fg_ref[...])
+    grad_mid = cot_ref[...].astype(F32) + norm_back(ghid, mid_hat, mid_istd, gain_f)
     gb_ag[n] = grad_mid.astype(BF16)
     gb_fin = narrow_gather(gb_ag)
     acc8[...] = jnp.zeros_like(acc8)
@@ -590,7 +593,7 @@
     lat_nf[0] = out_l
     here(lat_nf.at[0], out_lat)
     glat = glat_fin()
-    g_lat = grad_mid + norm_back(glat, lat_hat, lat_istd, lg_ref[...])
+    g_lat = grad_mid + norm_back(glat, lat_hat, lat_istd, gain_l)
     lat_nf[1] = g_lat.astype(BF16)
     here(lat_nf.at[1], out_gl)
     stat[FRAMES_MAX + 2 : FRAMES_MAX + 3, :] = jnp.sum(glat * lat_hat, axis=0, keepdims=True)
@@ -600,14 +603,14 @@
         gq_fwd(k)
     att_fin()
     sgb_fin()
-    o_o[...] = tn(att_g[...], sl_rc[3])
+    o_o[...] = tn(sl_rc[3], att_g[...])
     here(o_o, out_o)
     act_fin()
     scot_fin()
 
     def down_step(j, carry):
-        r = al(j * 256, 256)
-        o_down[pl.ds(r, 256), :] = tn(act_g[:, pl.ds(r, 256)], sl_rc[1])
+        cs = pl.ds(al(j * 256, 256), 256)
+        o_down[:, cs] = tn(sl_rc[1], act_g[:, cs])
         return carry
 
     lax.fori_loop(0, F // 256, down_step, 0)
@@ -690,6 +693,58 @@
     sem_counts.update(counters)
 
 
+def finish_kernel(p, pieces, *refs):
+    src, dst, buf, sem_in, sem_out = refs[:9], refs[9:24], refs[24:33], refs[33], refs[34]
+    V, C = p.V, p.C
+    loads = []
+    for i in range(9):
+        count = src[i].shape[0] // pieces[i]
+        for c in range(pieces[i]):
+            at = pl.ds(c * count, count)
+            d = pltpu.make_async_copy(src[i].at[at, :], buf[i].at[at, :], sem_in.at[len(loads)])
+            d.start()
+            loads.append((i, at, d))
+    stores = []
+
+    def store(a, b):
+        d = pltpu.make_async_copy(a, b, sem_out.at[len(stores)])
+        d.start()
+        stores.append(d)
+
+    first = {0: 0, 1: 1, 2: 2, 4: 10, 5: 11, 6: 12, 7: 13, 8: 14}
+    for i, at, d in loads:
+        d.wait()
+        if i == 3:
+            store(buf[3].at[pl.ds(0, FRAMES_MAX), :], dst[3])
+            for k in range(6):
+                store(buf[3].at[FRAMES_MAX + k], dst[4 + k])
+        elif i == 5 and C % LANES == 0:
+            for k in range(2):
+                store(buf[5].at[:, pl.ds(k * C, C)], dst[11].at[:, k, :])
+        else:
+            store(buf[i].at[at, :], dst[first[i]].at[at, :])
+    for d in stores:
+        d.wait()
+
+
+def finish(p, outs):
+    sds = jax.ShapeDtypeStruct
+    hbm = pl.BlockSpec(memory_space=pl.ANY)
+    pieces = [1, 4, 1, 1, 1, 1, 1, 2, 2]
+    shapes = [sds(a.shape, a.dtype) for a in outs]
+    vec = [sds((FRAMES_MAX, p.V), F32)] + [sds((p.V,), F32)] * 6
+    res = pl.pallas_call(
+        functools.partial(finish_kernel, p, pieces),
+        out_shape=tuple(shapes[:3] + vec + [shapes[4], sds((p.S, 2, p.C), F32) if p.C % LANES == 0 else shapes[5]] + shapes[6:]),
+        in_specs=[hbm] * 9,
+        out_specs=[hbm] * 15,
+        scratch_shapes=[pltpu.VMEM(a.shape, a.dtype) for a in outs]
+        + [pltpu.SemaphoreType.DMA((sum(pieces),)), pltpu.SemaphoreType.DMA((sum(pieces) + 7,))],
+        compiler_params=pltpu.CompilerParams(has_side_effects=True),
+    )(*outs)
+    return res[0], res[1], res[2], res[3:10], res[10], res[11].reshape(p.S, 2, p.C), res[12], res[13], res[14]
+
+
 def make_body(mesh):
     def body(
         media_feats, latents, frame_counts, media_mask, time_embed, media_gain, media_bias, latent_gain,
@@ -702,7 +757,6 @@
         vm = pl.BlockSpec(memory_space=pltpu.VMEM)
         hbm = pl.BlockSpec(memory_space=pl.ANY)
         smem = pl.BlockSpec(memory_space=pltpu.SMEM)
-        row = lambda v: v.reshape(1, D)
         sds = jax.ShapeDtypeStruct
         vmem = pltpu.VMEM
         scratch = [
@@ -752,8 +806,8 @@
             vmem((N, 16, V), F32),
             vmem((N, 16, V), F32),
             vmem((S, F), F32),
-            vmem((F, S), F32),
-            vmem((C, S), F32),
+            vmem((S, F), F32),
+            vmem((S, C), F32),
             vmem((S, C), F32),
             vmem((S, 2 * C), F32),
             vmem((16, V), F32),
@@ -770,11 +824,11 @@
                 sds((16, V), F32),
                 sds((S, C), F32),
                 sds((S, 2 * C), F32),
-                sds((C, S), F32),
+                sds((S, C), F32),
                 sds((S, F), F32),
-                sds((F, S), F32),
+                sds((S, F), F32),
             ),
-            in_specs=[hbm, vm, smem, vm, vm, vm, vm, vm, vm, vm, vm, hbm, hbm, vm, hbm, hbm, vm],
+            in_specs=[hbm, vm, smem, vm, vm, vm, vm, vm, vm, vm, vm, hbm, vm, hbm, hbm, hbm, vm],
             out_specs=[hbm] * 9,
             scratch_shapes=scratch,
             compiler_params=pltpu.CompilerParams(
@@ -782,15 +836,11 @@
             ),
         )(
             media_feats[0], latents[0], frame_counts, media_mask.reshape(p.M // LANES, LANES), time_embed,
-            row(media_gain), row(media_bias), row(latent_gain), row(latent_bias), row(ffn_gain), row(ffn_bias),
-            query_weight, keyval_weight.reshape(S, 2 * C), output_weight, up_weight, down_weight, cotangent[0],
+            media_gain, media_bias, latent_gain, latent_bias, ffn_gain, ffn_bias,
+            query_weight, keyval_weight, output_weight.T, up_weight, down_weight, cotangent[0],
         )
-        lat, gm, gl, vec, gq, gkv, go, gup, gdown = outs
-        return (
-            lat[None], gm[None], gl[None], vec[:FRAMES_MAX], vec[FRAMES_MAX], vec[FRAMES_MAX + 1],
-            vec[FRAMES_MAX + 2], vec[FRAMES_MAX + 3], vec[FRAMES_MAX + 4], vec[FRAMES_MAX + 5], gq,
-            gkv.reshape(S, 2, C), go, gup, gdown,
-        )
+        lat, gm, gl, vec, gq, gkv, go, gup, gdown = finish(p, outs)
+        return (lat[None], gm[None], gl[None]) + tuple(vec) + (gq, gkv, go.T, gup, gdown.T)
 
     return body
 

time: 235 us -> 217 us (0.923)
  local copies, waits for them, and re-layouts: 23 us -> 0 us
  Pallas kernels: 210 us -> 215 us
    unnamed x23 -> x0, local copies, waits for them, and re-layouts: 11.4 us -> none
    reshape x7 -> x0, local copies, waits for them, and re-layouts: 8.89 us -> none  [the longest x6 7.76 us: body(): row = lambda v: v.reshape(1, D)]
    pallas_call x0 -> x1, Pallas kernels: none -> 5.06 us  [finish(): pl.pallas_call(functools.partial(finish_kernel, p, pieces), out_shape=tup...]
where the time goes in v3:
time: 217 us
  Pallas kernels  215 us (99%)
    pallas_call x1, Pallas kernels, body(): pl.pallas_call(functools.partial(body_kernel, p, {}), out_shape=(sds((Lo,...  210 us
    pallas_call x1, Pallas kernels, finish(): pl.pallas_call(functools.partial(finish_kernel, p, pieces), out_shape=tup...  5.06 us

profile of v3, /device:TPU:0, one launch (start us, length us, event | category | flops | bytes accessed | tf_op | source)
XLA Modules:
  0.0 217.0 jit_solution(7352238548725917503)
XLA Ops:
  1.3 210.4 %shard_map.280 = (bf16[16,1536]{1,0:T(8,128)(2,1)}, bf16[512,1536]{1,0:T(8,128)(2,1)}, bf16[16,1536]{1,0:T(8,128)(2,1)}, f32[16,48]{1,0:T(8,128)}, f32[192,384]{...) custom-call(bf16[512,1536]{1,0:T(8,128)(2,1)} %bitcast.10, ...), custom_call_target="tpu_custom_call" | custom-call | tf_op jit(solution)/shard_map/pallas_call | solution.py:818
  211.7 5.1 %shard_map.281 = (bf16[16,1536]{1,0:T(8,128)(2,1)}, bf16[512,1536]{1,0:T(8,128)(2,1)}, bf16[16,1536]{1,0:T(8,128)(2,1)}, f32[8,48]{1,0:T(8,128)}, f32[48]{0:T(12...) custom-call(bf16[16,1536]{1,0:T(8,128)(2,1)} %get-tuple-element.39.r, ...), custom_call_target="tpu_custom_call" | custom-call | tf_op jit(solution)/shard_map/pallas_call | solution.py:736

commit v4 on v3

--- a/solution.py
+++ b/solution.py
@@ -72,7 +72,6 @@
         self.R = self.HL * self.L
         self.CH = 128
         self.NC = self.Mo // self.CH
-        self.reuse = self.F == self.D and self.X * self.Mo <= self.D
 
 
 def body_kernel(p, sem_counts, *refs):
@@ -83,7 +82,7 @@
         media, x_all, kvw, wq, wot, up, down, kv, st, pt, pn, gpair, mt, te32, mean_s, istd_s,
         lat_nf, lat_ag, cot_ag, cnt_ag,
         rs_st, rs_rc, hid_ag, gb_ag, mate_st, mate_rc, x_st, x_rc, own_sum,
-        kvg, kvg_y, kvg_z, act_g, pre_g, att_g, gq_g, sl_st, sl_rc, ga, acc8, stat, vec_st, vec_rc, vec2_st, vec2_rc,
+        kvg_y, kvg_z, act_own, pre_own, hid_g, cot_g, att_g, gq_g, sl_st, sl_rc, cot_sl, hid_sl, ga, acc8, stat, vec_st, vec_rc, vec2_st, vec2_rc,
         o_up, o_down, o_o, o_q, o_kv, o_vec, ssem, rsem, lsem,
     ) = refs
     N, W, X, W2 = p.N, p.W, p.X, p.W2
@@ -101,8 +100,7 @@
         ref[...].reshape(1, D) for ref in (mg_ref, mb_ref, lg_ref, lb_ref, fg_ref, fb_ref)
     )
 
-    if p.reuse:
-        mate_st, x_st = up, down
+    kvg = kv
 
     counters = {"s": 0, "r": 0, "l": 0}
     sends = []
@@ -119,6 +117,7 @@
         )
         d.start()
         sends.append(d)
+        return d
 
     def got(dst, recv):
         pltpu.make_async_remote_copy(
@@ -154,9 +153,14 @@
     down_in = here(down_h, down, False)
     up_in = here(up_h, up, False)
 
-    wkv = wkv_ref[...].astype(F32)
-    kvw[pl.ds(al(w * S, 16), S), 0:C] = wkv[:, 0, :].astype(BF16)
-    kvw[pl.ds(al(w * S, 16), S), C : 2 * C] = wkv[:, 1, :].astype(BF16)
+    def own_kv(i, carry):
+        v = wkv_ref[pl.ds(i * 16, 16)].astype(F32)
+        at = pl.ds(al(w * S + i * 16, 16), 16)
+        kvw[at, 0:C] = v[:, 0, :].astype(BF16)
+        kvw[at, C : 2 * C] = v[:, 1, :].astype(BF16)
+        return carry
+
+    lax.fori_loop(0, S // 16, own_kv, 0)
 
     barrier = pltpu.get_barrier_semaphore()
     for k in range(1, N):
@@ -165,13 +169,17 @@
         pl.semaphore_signal(barrier, inc=1, device_id={"wide": wpeer(k)}, device_id_type=MESH)
     pl.semaphore_wait(barrier, N - 1 + W - 1)
 
-    def wide_gather(src, buf, count):
-        at = lambda b: rows(buf, al(b * count, 16), count)
+    def wide_gather(src, at, link_y=True):
         direct = new("r", W2)
         fwd = new("r", W2)
         for k in range(1, W2):
             put(src, at(w), direct + k, "wide", wpeer(2 * k))
-        put(src, at(w), direct, "wide", partner)
+
+        def to_partner():
+            put(src, at(w), direct, "wide", partner)
+
+        if link_y:
+            to_partner()
 
         def forward(k):
             b = wsrc(2 * k)
@@ -184,15 +192,62 @@
                 b = lax.rem(partner + W - 2 * k, W)
                 got(at(b), fwd + k)
 
-        return forward, finish
+        return (forward, finish) if link_y else (forward, finish, to_partner)
+
+    def blocks(buf, count):
+        return lambda b: rows(buf, al(b * count, 16), count)
+
+    half_of = lambda c: pl.ds(al(c * (L // 2), 16), L // 2)
+    mine_half, mate_half = half_of(core), half_of(1 - core)
+
+    def hand_over(buf, base):
+        for k in range(1, W):
+            at = buf.at[wsrc(k), mine_half, :]
+            put(at, at, base + k, "narrow", mate)
+
+        def finish():
+            for k in range(1, W):
+                got(buf.at[wsrc(k), mate_half, :], base + k)
+
+        return finish
+
+    def row_gather(buf):
+        at = lambda b: buf.at[b, mine_half, :]
+        forward, finish = wide_gather(at(w), at)
+        base = new("r", W)
+
+        def share():
+            finish()
+            return hand_over(buf, base)
+
+        return forward, share
+
+    def spread(which, value):
+        for b in range(W):
+            sl_st[which, b] = value[:, b * S : (b + 1) * S]
+        base = new("r", W)
+        base2 = new("r", W)
+        for k in range(1, W):
+            put(
+                sl_st.at[which, wpeer(k), mine_half, :], sl_rc.at[which, w, mine_half, :],
+                base + k, "wide", wpeer(k),
+            )
+        sl_rc[which, w] = sl_st[which, w]
+
+        def share():
+            for k in range(1, W):
+                got(sl_rc.at[which, wsrc(k), mine_half, :], base + k)
+            return hand_over(sl_rc.at[which], base2)
+
+        return share
 
     own_w = [
         here(wq_h, rows(wq, al(w * S, 16), S), False),
         here(wot_h, rows(wot, al(w * S, 16), S), False),
     ]
-    kv_fwd, kv_fin = wide_gather(rows(kvw, al(w * S, 16), S), kvw, S)
-    q_fwd, q_fin = wide_gather(wq_h, wq, S)
-    o_fwd, o_fin = wide_gather(wot_h, wot, S)
+    kv_fwd, kv_fin = wide_gather(rows(kvw, al(w * S, 16), S), blocks(kvw, S))
+    q_fwd, q_fin = wide_gather(wq_h, blocks(wq, S))
+    o_fwd, o_fin, o_partner = wide_gather(wot_h, blocks(wot, S), False)
 
     lat = lat_ref[...].astype(F32)
     lat_mean, lat_istd, lat_hat = norm_stats(lat)
@@ -266,32 +321,14 @@
         put(cnt_ag.at[w], cnt_ag.at[w], cnt_base + k, "wide", wpeer(k))
 
     kv_fwd(1)
-    for k in range(2, W2):
-        kv_fwd(k)
-    media_forward(0)
-
-    def spread(which, value):
-        for b in range(W):
-            sl_st[which, b * L : (b + 1) * L, :] = value[:, b * S : (b + 1) * S]
-        base = new("r", W)
-        at = lambda ref, b: ref.at[which, pl.ds(al(b * L, 16), L), :]
-        for k in range(1, W):
-            put(at(sl_st, wpeer(k)), at(sl_rc, w), base + k, "wide", wpeer(k))
-        sl_rc[which, pl.ds(al(w * L, 16), L), :] = sl_st[which, pl.ds(al(w * L, 16), L), :]
-
-        def finish():
-            for k in range(1, W):
-                got(at(sl_rc, wsrc(k)), base + k)
-
-        return finish
+    o_partner()
 
     lat_all = lat_fin()
     cot_all = cot_fin()
     x_all[M : M + L, :] = lat_all
     if KT > M + L:
         x_all[M + L : KT, :] = jnp.zeros((KT - M - L, D), BF16)
-    slat_fin = spread(0, lat_all)
-    scot_fin = spread(1, cot_all)
+    cot_g[w] = cot_all
 
     down_in.wait()
 
@@ -302,10 +339,12 @@
 
     lax.fori_loop(0, F // 256, act_grad, 0)
 
-    for k in range(1, W2):
-        q_fwd(k)
-    if NC > 1:
-        media_forward(1)
+    media_forward(0)
+    for k in range(2, W2):
+        kv_fwd(k)
+    for c in range(1, NC - 1):
+        media_forward(c)
+    q_fwd(1)
     for d in own_w:
         d.wait()
     kv_fin()
@@ -318,13 +357,30 @@
 
         lax.fori_loop(0, count // CH, step, 0)
 
+    def project_far(c):
+        for j in range(1, X):
+            block = lax.rem(xpos + X - j, X) * 2 + core
+            project(block * Mo + c * CH, CH)
+
+    def project_mate(c):
+        for j in range(1, X):
+            block = lax.rem(xpos + X - j, X) * 2 + 1 - core
+            got(m_rows(block, c), m_fwd + c * X + j)
+            project(block * Mo + c * CH, CH)
+
     project(n * Mo, Mo)
     project(M, KT - M)
-    for k in range(1, W2):
-        o_fwd(k)
     for c in range(NC):
         got(m_rows(mate, c), m_direct + c * X)
     project(mate * Mo, Mo)
+    for c in range(NC - 1):
+        project_far(c)
+        project_mate(c)
+    for k in range(2, W2):
+        q_fwd(k)
+    if NC > 1:
+        media_forward(NC - 1)
+    project_far(NC - 1)
     q_fin()
     q_act = nn(lat_all, wq[...]).astype(BF16).astype(F32)
     head_of = lax.div(lax.broadcasted_iota(jnp.int32, (L, C), 1), HEAD_DIM)
@@ -341,15 +397,9 @@
     q_big32 = per_head(q_act)
     q_big = q_big32.astype(BF16)
     q_big_t = q_big32.T.astype(BF16)
-    for c in range(2, NC):
-        media_forward(c)
-    for c in range(NC):
-        for j in range(1, X):
-            block = lax.rem(xpos + X - j, X) * 2 + core
-            project(block * Mo + c * CH, CH)
-            block = lax.rem(xpos + X - j, X) * 2 + 1 - core
-            got(m_rows(block, c), m_fwd + c * X + j)
-            project(block * Mo + c * CH, CH)
+    project_mate(NC - 1)
+    for k in range(1, W2 - 2):
+        o_fwd(k)
 
     KB = 128
 
@@ -391,10 +441,14 @@
         pn[:, pl.ds(r, KB)] = pr.T.astype(BF16)
         return carry
 
+    o_fwd(W2 - 2)
     lax.fori_loop(0, KT // KB, prob_step, 0)
     attn = from_heads(nn(pn[...], kv[:, C : 2 * C]))
     attn_low = attn.astype(BF16)
 
+    o_fwd(W2 - 1)
+    cot_fwd, cot_share = row_gather(cot_g)
+    slat_share = spread(0, lat_all)
     at_w = lambda ref: rows(ref, al(w * L, 16), L)
     att_g[pl.ds(al(w * L, 16), L), :] = attn_low
 
@@ -416,8 +470,7 @@
         for i in range(N):
             rs_st[slot, i, :, cols] = v[i * Lo : (i + 1) * Lo].astype(BF16)
 
-    for d in (o_fin,):
-        d()
+    o_fin()
 
     def branch_step(j, carry):
         r = al(j * 256, 256)
@@ -426,13 +479,15 @@
 
     lax.fori_loop(0, D // 256, branch_step, 0)
     branch_fin = narrow_sum(0, None)
-    att_fwd, att_fin = wide_gather(at_w(att_g), att_g, L)
     mid = lat + branch_fin()
     mid_mean, mid_istd, mid_hat = norm_stats(mid)
     hid_ag[n] = (mid_hat * gain_f + bias_f).astype(BF16)
     hid_fin = narrow_gather(hid_ag)
     up_in.wait()
     hid_all = hid_fin()
+    hid_g[w] = hid_all
+    hid_fwd, hid_share = row_gather(hid_g)
+    att_fwd, att_fin = wide_gather(at_w(att_g), blocks(att_g, L))
 
     own64 = pl.ds(al(w * L, 16), L)
 
@@ -441,12 +496,12 @@
         pre = nn(hid_all, up[:, cs])
         cdf = 0.5 * (1.0 + lax.erf(pre * (1.0 / math.sqrt(2.0))))
         density = jnp.exp(-0.5 * pre * pre) * (1.0 / math.sqrt(2.0 * math.pi))
-        act_g[own64, cs] = (pre * cdf).astype(BF16)
-        pre_g[own64, cs] = (ga[:, cs] * (cdf + pre * density)).astype(BF16)
+        act_own[:, cs] = (pre * cdf).astype(BF16)
+        pre_own[:, cs] = (ga[:, cs] * (cdf + pre * density)).astype(BF16)
         return carry
 
     lax.fori_loop(0, F // 256, ffn_step, 0)
-    gpre = pre_g[own64, :]
+    gpre = pre_own[...]
 
     def hid_back(j, carry):
         r = al(j * 256, 256)
@@ -455,18 +510,17 @@
 
     lax.fori_loop(0, D // 256, hid_back, 0)
     ghid_fin = narrow_sum(1, None)
-    act_fwd, act_fin = wide_gather(at_w(act_g), act_g, L)
-    pre_fwd, pre_fin = wide_gather(at_w(pre_g), pre_g, L)
-    act_own = act_g[own64, :]
+    act_all = act_own[...]
 
     def ffn_out(j, carry):
         cs = pl.ds(al(j * 256, 256), 256)
-        stage(2, cs, nn(act_own, down[:, cs]))
+        stage(2, cs, nn(act_all, down[:, cs]))
         return carry
 
     lax.fori_loop(0, D // 256, ffn_out, 0)
     ffn_fin = narrow_sum(2, None)
-    shid_fin = spread(2, hid_all)
+    for k in range(1, W2):
+        cot_fwd(k)
 
     ghid = ghid_fin()
     grad_mid = cot_ref[...].astype(F32) + norm_back(ghid, mid_hat, mid_istd, gain_f)
@@ -476,8 +530,7 @@
     stat[...] = jnp.zeros_like(stat)
     stat[FRAMES_MAX + 4 : FRAMES_MAX + 5, :] = jnp.sum(ghid * mid_hat, axis=0, keepdims=True)
     stat[FRAMES_MAX + 5 : FRAMES_MAX + 6, :] = jnp.sum(ghid, axis=0, keepdims=True)
-    for k in range(1, W2):
-        att_fwd(k)
+    hid_fwd(1)
     for k in range(1, W):
         got(cnt_ag.at[wsrc(k)], cnt_base + k)
     keys = cnt_ag[0]
@@ -486,6 +539,7 @@
     ent1 = ENT_COEF * float(W * M) / keys[0:1, :]
     ent = jnp.concatenate([ent1] * (R // LANES), axis=1)
     gb_all = gb_fin()
+    sgb_share = spread(1, gb_all)
 
     g_attn = nn(gb_all, wot[...]).astype(BF16).astype(F32)
     g_big32 = per_head(g_attn)
@@ -504,7 +558,50 @@
         gpair[pl.ds(r, KB), C : 2 * C] = nn(pr.astype(BF16), g_big).astype(BF16)
         return carry
 
-    lax.fori_loop(0, KT // KB, back_step, 0)
+    lax.fori_loop(0, KT // KB // 2, back_step, 0)
+    for k in range(2, W2):
+        hid_fwd(k)
+    lax.fori_loop(KT // KB // 2, KT // KB, back_step, 0)
+
+    gq = (from_heads(nn(pn[...], kv[:, 0:C])) * scale).astype(BF16)
+    gq_g[own64, :] = gq
+    gq_fwd, gq_fin = wide_gather(at_w(gq_g), blocks(gq_g, L))
+
+    H = W2 // 2
+    half = lax.div(w, 2)
+    order = [(lax.rem(half + k, H) + (1 - lax.div(half, H)) * H) for k in range(H)]
+    order += [(lax.rem(half + k, H) + lax.div(half, H) * H) for k in list(range(1, H)) + [0]]
+    y_base = new("r", W2)
+    z_base = new("r", W2)
+
+    def kvg_rows(first):
+        def step(j, carry):
+            r = al(first * (D // 2) + j * 256, 256)
+            kvg[pl.ds(r, 256), :] = tn(x_all[:, pl.ds(r, 256)], gpair[...]).astype(BF16)
+            return carry
+
+        lax.fori_loop(0, D // 512, step, 0)
+
+    def kvg_to_partner(i):
+        put(
+            rows(kvg, al((2 * order[i] + 1 - par) * S, 16), S), rows(kvg_y, i * S, S),
+            y_base + i, "wide", partner,
+        )
+
+    def kvg_step(i):
+        g = order[i]
+        got(rows(kvg_y, i * S, S), y_base + i)
+        mine = pl.ds(al((2 * g + par) * S, 16), S)
+        summed = kvg[mine, :].astype(F32) + kvg_y[i * S : (i + 1) * S, :].astype(F32)
+        if i < W2 - 1:
+            kvg[mine, :] = summed.astype(BF16)
+            put(kvg.at[mine, :], rows(kvg_z, i * S, S), z_base + i, "wide", 2 * g + par)
+        else:
+            o_kv[...] = summed
+
+    kvg_rows(1 - lax.div(half, H))
+    for i in range(H):
+        kvg_to_partner(i)
 
     mate_base = new("r", X * NC)
     xs_base = new("r", X * NC)
@@ -513,36 +610,42 @@
         r = al(block * Mo + c * CH, 16)
         return nt(gpair[pl.ds(r, CH), :], kvw[...])
 
+    mate_sent = {}
+
     def x_of(j):
         return lax.rem(xpos + j, X)
 
     def to_mate(j, c):
         b = x_of(j) * 2 + 1 - core
-        mate_st[(j * NC + c) * CH : (j * NC + c + 1) * CH, :] = part(b, c).astype(BF16)
-        piece = lambda ref: rows(ref, (j * NC + c) * CH, CH)
-        put(piece(mate_st), piece(mate_rc), mate_base + j * NC + c, "narrow", mate)
+        if c in mate_sent:
+            mate_sent[c].wait_send()
+            sends[:] = [d for d in sends if d is not mate_sent[c]]
+        mate_st[c * CH : (c + 1) * CH, :] = part(b, c).astype(BF16)
+        mate_sent[c] = put(
+            rows(mate_st, c * CH, CH), rows(mate_rc, (j * NC + c) * CH, CH), mate_base + j * NC + c, "narrow", mate
+        )
 
     def from_mate(j, c):
         i = (j * NC + c) * CH
         got(rows(mate_rc, i, CH), mate_base + j * NC + c)
         return part(x_of(j) * 2 + core, c) + mate_rc[i : i + CH, :].astype(F32)
 
-    for j in range(1, X):
-        for c in range(NC):
+    def rows_out(j, cs):
+        for c in cs:
             to_mate(j, c)
-        for c in range(NC):
+        for c in cs:
             i = ((j - 1) * NC + c) * CH
             x_st[i : i + CH, :] = from_mate(j, c).astype(BF16)
             put(
                 rows(x_st, i, CH), rows(x_rc, i, CH), xs_base + (j - 1) * NC + c,
                 "narrow", x_of(j) * 2 + core,
             )
-    for k in range(1, W2):
-        act_fwd(k)
-        pre_fwd(k)
-
-    gq = (from_heads(nn(pn[...], kv[:, 0:C])) * scale).astype(BF16)
-    gq_g[own64, :] = gq
+
+    rows_out(1, range(NC // 2))
+    kvg_rows(lax.div(half, H))
+    for i in range(H, W2):
+        kvg_to_partner(i)
+
     gpl = gpair[M : M + L, :]
 
     def lat_back(j, carry):
@@ -552,42 +655,56 @@
 
     lax.fori_loop(0, D // 256, lat_back, 0)
     glat_fin = narrow_sum(3, None)
-    gq_fwd, gq_fin = wide_gather(at_w(gq_g), gq_g, L)
-    sgb_fin = spread(3, gb_all)
-
-    def kvg_step(j, carry):
-        r = al(j * 256, 256)
-        kvg[pl.ds(r, 256), :] = tn(x_all[:, pl.ds(r, 256)], gpair[...]).astype(BF16)
-        return carry
-
-    lax.fori_loop(0, D // 256, kvg_step, 0)
-    y_base = new("r", W2)
-    z_base = new("r", W2)
-    kb = lambda g, q: rows(kvg, al((2 * g + q) * S, 16), S)
-    for g in range(W2):
-        put(kb(g, 1 - par), rows(kvg_y, g * S, S), y_base + g, "wide", partner)
-
+    rows_out(1, range(NC // 2, NC))
+    for j in range(2, X):
+        rows_out(j, range(NC))
+    for k in range(1, W2):
+        att_fwd(k)
+    slat_fin = slat_share()
+    cot_fin = cot_share()
+    hid_fin = hid_share()
+    sgb_fin = sgb_share()
     for c in range(NC):
         to_mate(0, c)
     for c in range(NC):
         own_sum[c * CH : (c + 1) * CH, :] = from_mate(0, c)
-
-    half = lax.div(w, 2)
-    for k in list(range(1, W2)) + [0]:
-        g = lax.rem(half + k, W2)
-        yr = rows(kvg_y, al(g * S, 16), S)
-        got(yr, y_base) if W2 == 1 else None
-        if W2 > 1:
-            pltpu.make_async_remote_copy(
-                yr, yr, ssem.at[0], rsem.at[y_base + g], device_id={"narrow": mate}, device_id_type=MESH
-            ).wait_recv()
-        mine = pl.ds(al((2 * g + par) * S, 16), S)
-        summed = kvg[mine, :].astype(F32) + kvg_y[pl.ds(al(g * S, 16), S), :].astype(F32)
-        if k:
-            kvg[mine, :] = summed.astype(BF16)
-            put(rows(kvg, al((2 * g + par) * S, 16), S), rows(kvg_z, k * S, S), z_base + k, "wide", 2 * g + par)
-        else:
-            o_kv[...] = summed
+    third = [i * W2 // 4 for i in range(5)]
+    for i in range(third[0], third[1]):
+        kvg_step(i)
+
+    cot_fin()
+    hid_fin()
+    pick = (
+        lax.broadcasted_iota(jnp.int32, (D, S), 0) == lax.broadcasted_iota(jnp.int32, (D, S), 1) + w * S
+    ).astype(F32).astype(BF16)
+    cot_rows = lambda: cot_g[...].reshape(W * L, D)
+    hid_rows = lambda: hid_g[...].reshape(W * L, D)
+
+    def pick_step(b, carry):
+        at = pl.ds(al(b * L, 16), L)
+        cot_sl[at, :] = nn(cot_g[b], pick).astype(BF16)
+        hid_sl[at, :] = nn(hid_g[b], pick).astype(BF16)
+        return carry
+
+    lax.fori_loop(0, W, pick_step, 0)
+
+    def unit_step(j, carry):
+        cs = pl.ds(al(j * 256, 256), 256)
+        pre = nn(hid_rows(), up[:, cs])
+        grad = nt(cot_rows(), down[cs, :])
+        cdf = 0.5 * (1.0 + lax.erf(pre * (1.0 / math.sqrt(2.0))))
+        density = jnp.exp(-0.5 * pre * pre) * (1.0 / math.sqrt(2.0 * math.pi))
+        o_down[:, cs] = tn(cot_sl[...], (pre * cdf).astype(BF16))
+        o_up[:, cs] = tn(hid_sl[...], (grad * (cdf + pre * density)).astype(BF16))
+        return carry
+
+    units = F // 256
+    for t in range(3):
+        lax.fori_loop(t * units // 3, (t + 1) * units // 3, unit_step, 0)
+        for i in range(third[t + 1], third[t + 2]):
+            kvg_step(i)
+    here(o_up, out_up)
+    here(o_down, out_down)
 
     out_l = (mid + ffn_fin()).astype(BF16)
     lat_nf[0] = out_l
@@ -603,31 +720,11 @@
         gq_fwd(k)
     att_fin()
     sgb_fin()
-    o_o[...] = tn(sl_rc[3], att_g[...])
+    o_o[...] = tn(sl_rc[1].reshape(W * L, S), att_g[...])
     here(o_o, out_o)
-    act_fin()
-    scot_fin()
-
-    def down_step(j, carry):
-        cs = pl.ds(al(j * 256, 256), 256)
-        o_down[:, cs] = tn(sl_rc[1], act_g[:, cs])
-        return carry
-
-    lax.fori_loop(0, F // 256, down_step, 0)
-    here(o_down, out_down)
-    pre_fin()
-    shid_fin()
-
-    def up_step(j, carry):
-        cs = pl.ds(al(j * 256, 256), 256)
-        o_up[:, cs] = tn(sl_rc[2], pre_g[:, cs])
-        return carry
-
-    lax.fori_loop(0, F // 256, up_step, 0)
-    here(o_up, out_up)
     gq_fin()
     slat_fin()
-    o_q[...] = tn(sl_rc[0], gq_g[...])
+    o_q[...] = tn(sl_rc[0].reshape(W * L, S), gq_g[...])
     here(o_q, out_q)
 
     gm_out = []
@@ -666,9 +763,9 @@
     v_base = new("r", W)
     for k in range(1, W):
         put(vec_st.at[wpeer(k)], vec_rc.at[k], v_base + k, "wide", wpeer(k))
-    for k in range(1, W2):
-        got(rows(kvg_z, k * S, S), z_base + k)
-        o_kv[...] += kvg_z[k * S : (k + 1) * S, :].astype(F32)
+    for i in range(W2 - 1):
+        got(rows(kvg_z, i * S, S), z_base + i)
+        o_kv[...] += kvg_z[i * S : (i + 1) * S, :].astype(F32)
     here(o_kv, out_kv)
     vs = vec_st[w]
     for k in range(1, W):
@@ -784,20 +881,23 @@
             vmem((4, N, Lo, D), BF16),
             vmem((N, Lo, D), BF16),
             vmem((N, Lo, D), BF16),
-            vmem((8, LANES) if p.reuse else (X * Mo, D), BF16),
+            vmem((Mo, D), BF16),
             vmem((X * Mo, D), BF16),
-            vmem((8, LANES) if p.reuse else ((X - 1) * Mo, D), BF16),
+            vmem(((X - 1) * Mo, D), BF16),
             vmem(((X - 1) * Mo, D), BF16),
             vmem((Mo, D), F32),
-            vmem((D, 2 * C), BF16),
             vmem((W2 * S, 2 * C), BF16),
             vmem((W2 * S, 2 * C), BF16),
-            vmem((W * L, F), BF16),
-            vmem((W * L, F), BF16),
+            vmem((L, F), BF16),
+            vmem((L, F), BF16),
+            vmem((W, L, D), BF16),
+            vmem((W, L, D), BF16),
             vmem((W * L, C), BF16),
             vmem((W * L, C), BF16),
-            vmem((4, W * L, S), BF16),
-            vmem((4, W * L, S), BF16),
+            vmem((2, W, L, S), BF16),
+            vmem((2, W, L, S), BF16),
+            vmem((W * L, S), BF16),
+            vmem((W * L, S), BF16),
             vmem((L, F), F32),
             vmem((24, D), F32),
             vmem((16, D), F32),

time: 217 us -> 183 us (0.84)
  Pallas kernels: 215 us -> 181 us
    pallas_call x1, Pallas kernels: 210 us -> 176 us  [body(): pl.pallas_call(functools.partial(body_kernel, p, {}), out_shape=(sds((Lo,...]
where the time goes in v4:
time: 183 us
  Pallas kernels  181 us (99%)
    pallas_call x1, Pallas kernels, body(): pl.pallas_call(functools.partial(body_kernel, p, {}), out_shape=(sds((Lo,...  176 us
    pallas_call x1, Pallas kernels, finish(): pl.pallas_call(functools.partial(finish_kernel, p, pieces), out_shape=tup...  5.06 us

profile of v4, /device:TPU:0, one launch (start us, length us, event | category | flops | bytes accessed | tf_op | source)
XLA Modules:
  0.0 182.7 jit_solution(12524646405045607423)
XLA Ops:
  1.3 176.1 %shard_map.280 = (bf16[16,1536]{1,0:T(8,128)(2,1)}, bf16[512,1536]{1,0:T(8,128)(2,1)}, bf16[16,1536]{1,0:T(8,128)(2,1)}, f32[16,48]{1,0:T(8,128)}, f32[192,384]{...) custom-call(bf16[512,1536]{1,0:T(8,128)(2,1)} %bitcast.10, ...), custom_call_target="tpu_custom_call" | custom-call | tf_op jit(solution)/shard_map/pallas_call | solution.py:918
  177.4 5.1 %shard_map.281 = (bf16[16,1536]{1,0:T(8,128)(2,1)}, bf16[512,1536]{1,0:T(8,128)(2,1)}, bf16[16,1536]{1,0:T(8,128)(2,1)}, f32[8,48]{1,0:T(8,128)}, f32[48]{0:T(12...) custom-call(bf16[16,1536]{1,0:T(8,128)(2,1)} %get-tuple-element.39.r, ...), custom_call_target="tpu_custom_call" | custom-call | tf_op jit(solution)/shard_map/pallas_call | solution.py:833

commit v5 on v4

--- a/solution.py
+++ b/solution.py
@@ -104,6 +104,7 @@
 
     counters = {"s": 0, "r": 0, "l": 0}
     sends = []
+    sends_if = []
     local = []
 
     def new(kind, count=1):
@@ -119,6 +120,20 @@
         sends.append(d)
         return d
 
+    def put_if(cond, src, dst, recv, peer):
+        sem = ssem.at[new("s")]
+
+        def copy():
+            return pltpu.make_async_remote_copy(
+                src, dst, sem, rsem.at[recv], device_id={"wide": peer}, device_id_type=MESH
+            )
+
+        @pl.when(cond)
+        def _():
+            copy().start()
+
+        sends_if.append((cond, copy))
+
     def got(dst, recv):
         pltpu.make_async_remote_copy(
             dst, dst, ssem.at[0], rsem.at[recv], device_id={"narrow": mate}, device_id_type=MESH
@@ -169,17 +184,56 @@
         pl.semaphore_signal(barrier, inc=1, device_id={"wide": wpeer(k)}, device_id_type=MESH)
     pl.semaphore_wait(barrier, N - 1 + W - 1)
 
-    def wide_gather(src, at, link_y=True):
+    pos = lax.div(w, 2)
+    above, below = pos < W2 - 1, pos > 0
+
+    def wide_gather(src, at, start=True):
+        across = new("r")
+        up, down, up_across, down_across = (new("r", W2) for _ in range(4))
+
+        def begin():
+            put_if(above, src, at(w), up + 1, wpeer(2))
+            put_if(below, src, at(w), down + 1, wsrc(2))
+            put(src, at(w), across, "wide", partner)
+
+        if start:
+            begin()
+
+        def forward(k):
+            for arrives, onward, b, flow, to, flow_across in (
+                (pos >= k, above, wsrc(2 * k), up, wpeer(2), up_across),
+                (pos + k < W2, below, wpeer(2 * k), down, wsrc(2), down_across),
+            ):
+
+                @pl.when(arrives)
+                def _(b=b, flow=flow):
+                    got(at(b), flow + k)
+
+                if k < W2 - 1:
+                    put_if(arrives & onward, at(b), at(b), flow + k + 1, to)
+                put_if(arrives, at(b), at(b), flow_across + k, partner)
+
+        def finish():
+            got(at(partner), across)
+            for k in range(1, W2):
+
+                @pl.when(pos >= k)
+                def _(k=k):
+                    got(at(lax.rem(partner + W - 2 * k, W)), up_across + k)
+
+                @pl.when(pos + k < W2)
+                def _(k=k):
+                    got(at(lax.rem(partner + 2 * k, W)), down_across + k)
+
+        return (forward, finish) if start else (forward, finish, begin)
+
+    def small_gather(src, at):
         direct = new("r", W2)
         fwd = new("r", W2)
         for k in range(1, W2):
             put(src, at(w), direct + k, "wide", wpeer(2 * k))
 
-        def to_partner():
-            put(src, at(w), direct, "wide", partner)
-
-        if link_y:
-            to_partner()
+        put(src, at(w), direct, "wide", partner)
 
         def forward(k):
             b = wsrc(2 * k)
@@ -192,7 +246,7 @@
                 b = lax.rem(partner + W - 2 * k, W)
                 got(at(b), fwd + k)
 
-        return (forward, finish) if link_y else (forward, finish, to_partner)
+        return forward, finish
 
     def blocks(buf, count):
         return lambda b: rows(buf, al(b * count, 16), count)
@@ -213,7 +267,7 @@
 
     def row_gather(buf):
         at = lambda b: buf.at[b, mine_half, :]
-        forward, finish = wide_gather(at(w), at)
+        forward, finish = small_gather(at(w), at)
         base = new("r", W)
 
         def share():
@@ -247,7 +301,7 @@
     ]
     kv_fwd, kv_fin = wide_gather(rows(kvw, al(w * S, 16), S), blocks(kvw, S))
     q_fwd, q_fin = wide_gather(wq_h, blocks(wq, S))
-    o_fwd, o_fin, o_partner = wide_gather(wot_h, blocks(wot, S), False)
+    o_fwd, o_fin, o_begin = wide_gather(wot_h, blocks(wot, S), False)
 
     lat = lat_ref[...].astype(F32)
     lat_mean, lat_istd, lat_hat = norm_stats(lat)
@@ -304,6 +358,8 @@
             block = lax.rem(xpos + X - j, X) * 2 + core
             got(m_rows(block, c), m_direct + c * X + j)
             put(m_rows(block, c), m_rows(block, c), m_fwd + c * X + j, "narrow", mate)
+
+    kv_fwd(1)
 
     slot_frame = lax.div(lax.broadcasted_iota(jnp.int32, (M // LANES, LANES), 0), PATCHES // LANES)
     ok = (slot_frame < fc_ref[0]) & (mm_ref[...] > 0)
@@ -320,8 +376,10 @@
     for k in range(1, W):
         put(cnt_ag.at[w], cnt_ag.at[w], cnt_base + k, "wide", wpeer(k))
 
-    kv_fwd(1)
-    o_partner()
+    if W2 > 2:
+        kv_fwd(2)
+    o_begin()
+    media_forward(0)
 
     lat_all = lat_fin()
     cot_all = cot_fin()
@@ -339,12 +397,13 @@
 
     lax.fori_loop(0, F // 256, act_grad, 0)
 
-    media_forward(0)
-    for k in range(2, W2):
+    q_fwd(1)
+    for k in range(3, W2):
         kv_fwd(k)
     for c in range(1, NC - 1):
         media_forward(c)
-    q_fwd(1)
+    for k in range(2, W2):
+        q_fwd(k)
     for d in own_w:
         d.wait()
     kv_fin()
@@ -376,8 +435,7 @@
     for c in range(NC - 1):
         project_far(c)
         project_mate(c)
-    for k in range(2, W2):
-        q_fwd(k)
+    o_fwd(1)
     if NC > 1:
         media_forward(NC - 1)
     project_far(NC - 1)
@@ -398,7 +456,7 @@
     q_big = q_big32.astype(BF16)
     q_big_t = q_big32.T.astype(BF16)
     project_mate(NC - 1)
-    for k in range(1, W2 - 2):
+    for k in range(2, W2 - 1):
         o_fwd(k)
 
     KB = 128
@@ -441,12 +499,11 @@
         pn[:, pl.ds(r, KB)] = pr.T.astype(BF16)
         return carry
 
-    o_fwd(W2 - 2)
+    o_fwd(W2 - 1)
     lax.fori_loop(0, KT // KB, prob_step, 0)
     attn = from_heads(nn(pn[...], kv[:, C : 2 * C]))
     attn_low = attn.astype(BF16)
 
-    o_fwd(W2 - 1)
     cot_fwd, cot_share = row_gather(cot_g)
     slat_share = spread(0, lat_all)
     at_w = lambda ref: rows(ref, al(w * L, 16), L)
@@ -487,7 +544,7 @@
     hid_all = hid_fin()
     hid_g[w] = hid_all
     hid_fwd, hid_share = row_gather(hid_g)
-    att_fwd, att_fin = wide_gather(at_w(att_g), blocks(att_g, L))
+    att_fwd, att_fin = small_gather(at_w(att_g), blocks(att_g, L))
 
     own64 = pl.ds(al(w * L, 16), L)
 
@@ -565,7 +622,7 @@
 
     gq = (from_heads(nn(pn[...], kv[:, 0:C])) * scale).astype(BF16)
     gq_g[own64, :] = gq
-    gq_fwd, gq_fin = wide_gather(at_w(gq_g), blocks(gq_g, L))
+    gq_fwd, gq_fin = small_gather(at_w(gq_g), blocks(gq_g, L))
 
     H = W2 // 2
     half = lax.div(w, 2)
@@ -785,6 +842,12 @@
 
     for d in sends:
         d.wait_send()
+    for cond, copy in sends_if:
+
+        @pl.when(cond)
+        def _(copy=copy):
+            copy().wait_send()
+
     for d in local:
         d.wait()
     sem_counts.update(counters)
@@ -911,8 +974,8 @@
             vmem((S, C), F32),
             vmem((S, 2 * C), F32),
             vmem((16, V), F32),
-            pltpu.SemaphoreType.DMA((24 * W + 8 * N * p.NC + 64,)),
-            pltpu.SemaphoreType.DMA((24 * W + 8 * N * p.NC + 64,)),
+            pltpu.SemaphoreType.DMA((40 * W + 8 * N * p.NC + 64,)),
+            pltpu.SemaphoreType.DMA((40 * W + 8 * N * p.NC + 64,)),
             pltpu.SemaphoreType.DMA((64,)),
         ]
         outs = pl.pallas_call(

time: 183 us -> 167 us (0.913)
  Pallas kernels: 181 us -> 165 us
    pallas_call x1, Pallas kernels: 176 us -> 160 us  [body(): pl.pallas_call(functools.partial(body_kernel, p, {}), out_shape=(sds((Lo,...]
where the time goes in v5:
time: 167 us
  Pallas kernels  165 us (99%)
    pallas_call x1, Pallas kernels, body(): pl.pallas_call(functools.partial(body_kernel, p, {}), out_shape=(sds((Lo,...  160 us
    pallas_call x1, Pallas kernels, finish(): pl.pallas_call(functools.partial(finish_kernel, p, pieces), out_shape=tup...  5.06 us

profile of v5, /device:TPU:0, one launch (start us, length us, event | category | flops | bytes accessed | tf_op | source)
XLA Modules:
  0.0 166.7 jit_solution(16849568873111767413)
XLA Ops:
  1.3 160.1 %shard_map.280 = (bf16[16,1536]{1,0:T(8,128)(2,1)}, bf16[512,1536]{1,0:T(8,128)(2,1)}, bf16[16,1536]{1,0:T(8,128)(2,1)}, f32[16,48]{1,0:T(8,128)}, f32[192,384]{...) custom-call(bf16[512,1536]{1,0:T(8,128)(2,1)} %bitcast.10, ...), custom_call_target="tpu_custom_call" | custom-call | tf_op jit(solution)/shard_map/pallas_call | solution.py:981
  161.4 5.1 %shard_map.281 = (bf16[16,1536]{1,0:T(8,128)(2,1)}, bf16[512,1536]{1,0:T(8,128)(2,1)}, bf16[16,1536]{1,0:T(8,128)(2,1)}, f32[8,48]{1,0:T(8,128)}, f32[48]{0:T(12...) custom-call(bf16[16,1536]{1,0:T(8,128)(2,1)} %get-tuple-element.39.r, ...), custom_call_target="tpu_custom_call" | custom-call | tf_op jit(solution)/shard_map/pallas_call | solution.py:896

commit v6 on v5

--- a/solution.py
+++ b/solution.py
@@ -721,12 +721,14 @@
     cot_fin = cot_share()
     hid_fin = hid_share()
     sgb_fin = sgb_share()
+    third = [i * W2 // 4 for i in range(5)]
+    for i in range(third[0], third[1]):
+        kvg_step(i)
     for c in range(NC):
         to_mate(0, c)
     for c in range(NC):
         own_sum[c * CH : (c + 1) * CH, :] = from_mate(0, c)
-    third = [i * W2 // 4 for i in range(5)]
-    for i in range(third[0], third[1]):
+    for i in range(third[1], third[2]):
         kvg_step(i)
 
     cot_fin()
@@ -758,7 +760,7 @@
     units = F // 256
     for t in range(3):
         lax.fori_loop(t * units // 3, (t + 1) * units // 3, unit_step, 0)
-        for i in range(third[t + 1], third[t + 2]):
+        for i in range(third[min(t + 2, 4)], third[min(t + 3, 4)]):
             kvg_step(i)
     here(o_up, out_up)
     here(o_down, out_down)
@@ -807,7 +809,7 @@
             acc8[16:24, :] += fold8(dx)
             return carry
 
-        lax.fori_loop(0, CH // 16, back_rows, 0)
+        lax.fori_loop(0, CH // 16, back_rows, 0, unroll=2)
         stat[pl.ds(f, 1), :] += jnp.sum(acc8[16:24, :], axis=0, keepdims=True)
         acc8[16:24, :] = jnp.zeros((8, D), F32)
         here(rows(media, c * CH, CH), rows(out_gm, c * CH, CH))

time: 167 us -> 166 us (level)
  no operation moved by 1% of the time
where the time goes in v6:
time: 166 us
  Pallas kernels  164 us (99%)
    pallas_call x1, Pallas kernels, body(): pl.pallas_call(functools.partial(body_kernel, p, {}), out_shape=(sds((Lo,...  159 us
    pallas_call x1, Pallas kernels, finish(): pl.pallas_call(functools.partial(finish_kernel, p, pieces), out_shape=tup...  5.06 us

profile of v6, /device:TPU:0, one launch (start us, length us, event | category | flops | bytes accessed | tf_op | source)
XLA Modules:
  0.0 165.6 jit_solution(6639760589059271998)
XLA Ops:
  1.3 159.1 %shard_map.280 = (bf16[16,1536]{1,0:T(8,128)(2,1)}, bf16[512,1536]{1,0:T(8,128)(2,1)}, bf16[16,1536]{1,0:T(8,128)(2,1)}, f32[16,48]{1,0:T(8,128)}, f32[192,384]{...) custom-call(bf16[512,1536]{1,0:T(8,128)(2,1)} %bitcast.10, ...), custom_call_target="tpu_custom_call" | custom-call | tf_op jit(solution)/shard_map/pallas_call | solution.py:983
  160.4 5.1 %shard_map.281 = (bf16[16,1536]{1,0:T(8,128)(2,1)}, bf16[512,1536]{1,0:T(8,128)(2,1)}, bf16[16,1536]{1,0:T(8,128)(2,1)}, f32[8,48]{1,0:T(8,128)}, f32[48]{0:T(12...) custom-call(bf16[16,1536]{1,0:T(8,128)(2,1)} %get-tuple-element.39.r, ...), custom_call_target="tpu_custom_call" | custom-call | tf_op jit(solution)/shard_map/pallas_call | solution.py:898
